TPU v7x, 32 devices: a whole 2x2x4 slice. The times are simulated.
32 devices in a mesh: groups: 2 (over x), tensor: 16 (over z, y, core).
Axes of the slice: x: 2, y: 2, z: 4, core: 2. Of those that a mesh axis runs over, the one named last changes fastest.
Arguments:
- residual_in: bfloat16 [1024, 6144], P('groups', 'tensor'), parts along dimension 0
- norm_gain: bfloat16 [6144], P('tensor'), may hold values from 0.099609375 to 1.8984375
- final_gain: bfloat16 [6144], P('tensor'), may hold values from 0.099609375 to 1.8984375
- expert_ids: int32 [1024, 2], P('groups'), parts along dimension 0, may hold values from 0 to 3, all different within a row; in each aligned block of 512 rows (0 to 511, 512 to 1023, ...) at most 384 rows name the same one
- gate_values: float32 [1024, 2], P('groups'), parts along dimension 0, may hold values from 0.2 to 1
- w_gate: bfloat16 [6144, 32768], P(None, 'tensor'), may hold values from -0.078125 to 0.078125
- w_up: bfloat16 [6144, 32768], P(None, 'tensor'), may hold values from -0.078125 to 0.078125
- w_down: bfloat16 [32768, 6144], P('tensor')
- lm_head: bfloat16 [6144, 32768], P(None, 'tensor')
- target_ids: int32 [1024], P('groups'), parts along dimension 0, may hold values from 0 to 32767
- lengths: int32 [16], P('groups'), parts along dimension 0, may hold values from 1 to 64
Outputs:
- masked_logprob: float32 [1024], P(('groups', 'tensor')), parts along dimension 0
There are 2 independent parts, one for each index of `groups`. A program takes and returns all parts, laid end to end along the dimension named above; an argument that names none is the same for every part. Nothing has to cross between parts.
Inputs may be any that keep to these rules, and one draw needn't show every extreme that they name: `expert_ids`: no expert is named by more than 384 tokens of a frontier batch, a bound that some block reaches.
All inputs are finite; a program needn't handle non-finite values.
Results may differ from a plain program's by a relative error of at most 0.0055.
Values may be sent and summed in bfloat16 or wider, within the bound.
No kernel may reach another device: no remote copies, remote signals or barrier semaphores. Data moves between devices by JAX's collectives and lax.ppermute only.
A program may use at most 192 MiB of HBM per device.

v0:
```python
import functools
import jax
import jax.numpy as jnp
from jax import lax
from jax.experimental import pallas as pl
from jax.experimental.pallas import tpu as pltpu
from jax.sharding import PartitionSpec as P

D = 6144
EXPERTS = 4
EXP_FF = 8192
TOP = 2
SEQ = 64
CAP = 384


epsilon = 1e-05


def combined_all(array, axis, combine):
    everything = jax.tree.map(lambda part: lax.all_gather(part, axis), array)
    leading = jax.tree.map(lambda part: part[0], everything)

    def hop(k, so_far):
        return combine(so_far, jax.tree.map(lambda part: part[k], everything))

    return lax.fori_loop(1, lax.axis_size(axis), hop, leading)


def slots_of(expert_ids):
    flat_ids = expert_ids.reshape(-1)
    pairs = jnp.arange(flat_ids.shape[0], dtype=jnp.int32)
    before = (pairs[None, :] < pairs[:, None]) & (flat_ids[None, :] == flat_ids[:, None])
    return jnp.sum(before.astype(jnp.int32), axis=1).reshape(expert_ids.shape)


def slot_tokens(expert_ids, slot_index):
    slot_code = (expert_ids * CAP + slot_index).reshape(-1)
    owner = jnp.arange(slot_code.shape[0], dtype=jnp.int32) // TOP
    wanted = jnp.arange(EXPERTS * CAP, dtype=jnp.int32)
    matches = slot_code[None, :] == wanted[:, None]
    return jnp.sum(jnp.where(matches, owner[None, :] + 1, 0), axis=1) - 1


def normalize(values, squares_total, gain_vec):
    return (
        values / jnp.sqrt(squares_total[:, None] / D + epsilon) * gain_vec.astype(jnp.float32)
    ).astype(jnp.bfloat16)


def plain_body(
    residual_in,
    norm_gain,
    final_gain,
    expert_ids,
    gate_values,
    w_gate,
    w_up,
    w_down,
    lm_head,
    target_ids,
    lengths,
):
    tokens, feature_cols = residual_in.shape
    hidden_dev = w_gate.shape[1]
    per_expert = EXP_FF // hidden_dev
    expert_now = lax.axis_index("tensor") // per_expert
    stream = residual_in.astype(jnp.float32)
    in_total = lax.psum(jnp.sum(stream * stream, axis=1), "tensor")
    normed = normalize(stream, in_total, norm_gain)
    slot_index = slots_of(expert_ids)
    token_of = slot_tokens(expert_ids, slot_index)
    zero_bf = jnp.zeros((), jnp.bfloat16)
    own_slots = lax.dynamic_slice_in_dim(token_of, expert_now * CAP, CAP)
    occupied = own_slots >= 0
    safe_index = jnp.maximum(own_slots, 0)
    slot_rows = jnp.where(
        occupied[:, None], lax.all_gather(normed, "tensor", axis=1, tiled=True)[safe_index], zero_bf
    )
    gate_out = jnp.dot(slot_rows, w_gate, preferred_element_type=jnp.float32)
    up_out = jnp.dot(slot_rows, w_up, preferred_element_type=jnp.float32)
    hidden = (jax.nn.silu(gate_out) * up_out).astype(jnp.bfloat16)
    partial_value = jnp.dot(hidden, w_down, preferred_element_type=jnp.float32)
    weight_own = jnp.where(expert_ids == expert_now, gate_values, jnp.zeros_like(gate_values))
    weighted = (
        weight_own[:, 0:1] * partial_value[slot_index[:, 0]]
        + weight_own[:, 1:2] * partial_value[slot_index[:, 1]]
    )
    moe_cols = lax.psum_scatter(weighted, "tensor", scatter_dimension=1, tiled=True)
    mixture = stream + moe_cols
    out_total = lax.psum(jnp.sum(mixture * mixture, axis=1), "tensor")
    normed_out = normalize(mixture, out_total, final_gain)
    vocab_dev = lm_head.shape[1]
    logits = jnp.dot(
        lax.all_gather(normed_out, "tensor", axis=1, tiled=True),
        lm_head,
        preferred_element_type=jnp.float32,
    )
    row_max = jnp.max(logits, axis=1)
    row_total = jnp.sum(jnp.exp(logits - row_max[:, None]), axis=1)
    local_ids = target_ids - lax.axis_index("tensor") * vocab_dev
    vocab_cols = jnp.arange(vocab_dev, dtype=jnp.int32)
    picked = jnp.sum(jnp.where(vocab_cols[None, :] == local_ids[:, None], logits, 0.0), axis=1)

    def joined(earlier, later):
        merged_max = jnp.maximum(earlier[0], later[0])
        merged_total = earlier[1] * jnp.exp(earlier[0] - merged_max) + later[1] * jnp.exp(
            later[0] - merged_max
        )
        return (merged_max, merged_total, earlier[2] + later[2])

    merged_max, merged_total, target_logit = combined_all(
        (row_max, row_total, picked), "tensor", joined
    )
    logprob = target_logit - merged_max - jnp.log(merged_total)
    rows_dev = tokens // lax.axis_size("tensor")
    first_row = lax.axis_index("tensor") * rows_dev
    own_rows = lax.dynamic_slice_in_dim(logprob, first_row, rows_dev)
    position = first_row + jnp.arange(rows_dev, dtype=jnp.int32)
    in_length = position % SEQ < lengths[position // SEQ]
    return jnp.where(in_length, own_rows, jnp.zeros_like(own_rows)).astype(jnp.float32)

TIERS = ((288, 224), (352, 272))
CHUNKS = ((0,), (1, 3), (2,))
VMEM = pl.BlockSpec(memory_space=pltpu.VMEM)
BF = jnp.bfloat16
F32 = jnp.float32


def send(array, pairs):
    return lax.ppermute(array, "tensor", pairs)


def xor_pairs(mask):
    return [(i, i ^ mask) for i in range(16)]


def plane_pairs(k):
    return [(i, ((i >> 2) + k) % 4 * 4 + (i & 3)) for i in range(16)]


def after(value, *others):
    return lax.optimization_barrier((value, *others))[0]


def params(mebibytes):
    return pltpu.CompilerParams(vmem_limit_bytes=mebibytes * 1024 * 1024)


def load_kernel(w_ref, after_ref, out_ref, token_ref, sem):
    copy = pltpu.make_async_copy(w_ref, out_ref, sem)
    copy.start()
    copy.wait()
    token_ref[...] = jnp.zeros_like(token_ref)


def resident(weight, ready):
    weight = pltpu.with_memory_space_constraint(weight, pltpu.HBM)
    return pl.pallas_call(
        load_kernel,
        in_specs=[pl.BlockSpec(memory_space=pltpu.HBM), pl.BlockSpec(memory_space=pl.ANY)],
        out_specs=[VMEM, VMEM],
        out_shape=[
            pltpu.VMEM(weight.shape, weight.dtype),
            jax.ShapeDtypeStruct((8, 128), F32),
        ],
        scratch_shapes=[pltpu.SemaphoreType.DMA],
        compiler_params=params(1),
        cost_estimate=pl.CostEstimate(
            flops=0, transcendentals=0, bytes_accessed=4 * weight.size
        ),
    )(weight, ready)


def cost(rows, inner, cols, other_bytes):
    return pl.CostEstimate(
        flops=2 * rows * inner * cols,
        transcendentals=0,
        bytes_accessed=2 * inner * cols + other_bytes,
    )


def route_kernel(where_ref, lengths_ref, ids_ref, gates_ref, slots_ref, gate_ref, need_ref, used_ref):
    tokens = ids_ref.shape[1]
    spot = lax.broadcasted_iota(jnp.int32, (1, tokens), 1)
    cand = lax.shift_right_logical(spot, SEQ.bit_length() - 1)
    size = jnp.zeros_like(spot)
    start = jnp.zeros_like(spot)
    alive = jnp.int32(0)
    for c in range(lengths_ref.shape[0]):
        size = jnp.where(cand == c, lengths_ref[c], size)
        start = jnp.where(cand == c, alive, start)
        alive = alive + lengths_ref[c]
    step = spot - cand * SEQ
    live = step < size
    used_ref[...] = jnp.zeros_like(used_ref)
    for k in range(EXPERTS):
        expert = lax.rem(where_ref[0] + k, EXPERTS)
        first = (ids_ref[0:1, :] == expert) & live
        second = (ids_ref[1:2, :] == expert) & live
        used_ref[k : k + 1, :] = jnp.where(first | second, 1.0, 0.0)
        if k == 0:
            gate_ref[...] = jnp.where(first, gates_ref[0:1, :], 0.0) + jnp.where(
                second, gates_ref[1:2, :], 0.0
            )
    used = used_ref[...]
    source = lax.broadcasted_iota(jnp.int32, (tokens, tokens), 0)
    target = lax.broadcasted_iota(jnp.int32, (tokens, tokens), 1)
    earlier = jnp.where(source < target, 1.0, 0.0).astype(BF)
    rank = jnp.dot(used.astype(BF), earlier, preferred_element_type=F32)
    slots_ref[...] = jnp.where(used > 0.0, rank.astype(jnp.int32), -1)
    slots_ref[4:5, :] = jnp.where(live, start + step, -1)
    fullest = jnp.max(jnp.sum(used, axis=1, keepdims=True))
    need = jnp.float32(0.0)
    for rows, slots in TIERS:
        over = (alive > rows) | (fullest > float(slots))
        need = need + jnp.where(over, 1.0, 0.0)
    need_ref[...] = jnp.full(need_ref.shape, need, F32)


def route(plane, lengths, ids, gates):
    tokens = ids.shape[1]
    smem = pl.BlockSpec(memory_space=pltpu.SMEM)
    vmem = pl.BlockSpec(memory_space=pltpu.VMEM)
    return pl.pallas_call(
        route_kernel,
        in_specs=[smem, smem, vmem, vmem],
        out_specs=[vmem] * 3,
        out_shape=[
            jax.ShapeDtypeStruct((8, tokens), jnp.int32),
            jax.ShapeDtypeStruct((1, tokens), F32),
            jax.ShapeDtypeStruct((8, 128), F32),
        ],
        scratch_shapes=[pltpu.VMEM((8, tokens), F32)],
        compiler_params=params(16),
    )(plane.reshape(1), lengths, ids, gates)


def dispatch_kernel(slot_ref, x_ref, gain_ref, s0, s1, s2, s3, xc_ref):
    x = x_ref[...]
    scaled = (x.astype(F32) * gain_ref[...].astype(F32)).astype(BF)
    tokens = x.shape[0]
    for k, out in enumerate((s0, s1, s2, s3)):
        rows = out.shape[0]
        spots = lax.broadcasted_iota(jnp.int32, (rows, tokens), 0)
        chosen = jnp.where(slot_ref[k : k + 1, :] == spots, 1.0, 0.0).astype(BF)
        out[...] = jnp.dot(chosen, scaled, preferred_element_type=F32).astype(BF)
    rows = xc_ref.shape[0]
    spots = lax.broadcasted_iota(jnp.int32, (rows, tokens), 0)
    chosen = jnp.where(slot_ref[4:5, :] == spots, 1.0, 0.0).astype(BF)
    xc_ref[...] = jnp.dot(chosen, x, preferred_element_type=F32).astype(BF)


def dispatch(slot_rows, x, gain, slots, live_rows):
    cols = x.shape[1]
    block = jax.ShapeDtypeStruct((slots, cols), BF)
    return pl.pallas_call(
        dispatch_kernel,
        out_shape=[block] * 4 + [jax.ShapeDtypeStruct((live_rows, cols), BF)],
        compiler_params=params(16),
    )(slot_rows, x, gain)


def place(where_ref, blocks, wide_ref):
    own, across, *core = blocks
    rows, cols = wide_ref.shape[0], own.shape[1]
    count = own.shape[0] // rows
    for g in range(count):
        pieces = ((own, g), (across, g), (core[0], g), (core[-1], g if len(core) == 2 else count + g))
        for quarter, (block, piece) in enumerate(pieces):
            at = pl.multiple_of((g * 4 + where_ref[quarter]) * cols, 128)
            wide_ref[:, pl.ds(at, cols)] = block[piece * rows : (piece + 1) * rows, :]


def whole_specs(arrays):
    return [pl.BlockSpec(array.shape, lambda n, w: (0, 0)) for array in arrays]


def product(wide, weights):
    depth = weights[0].shape[0]
    value = None
    for j, w in enumerate(weights):
        part = jnp.dot(
            wide[:, j * depth : (j + 1) * depth], w[...], preferred_element_type=F32
        )
        value = part if value is None else value + part
    return value


def resident_product(where_ref, wide, weight, n, tile):
    depth = weight.shape[0] // 4
    value = None
    for j in range(wide.shape[1] // depth):
        first = pl.multiple_of(where_ref[4 + j] * depth, 128)
        part = jnp.dot(
            wide[:, j * depth : (j + 1) * depth],
            weight[pl.ds(first, depth), pl.ds(pl.multiple_of(n * tile, 128), tile)],
            preferred_element_type=F32,
        )
        value = part if value is None else value + part
    return value


def weight_specs(count, depth, tile):
    return [
        pl.BlockSpec((depth, tile), functools.partial(lambda j, n, w: (w[4 + j], n), j))
        for j in range(count)
    ]


def by_slot(slot_ref, values, slots):
    spots = lax.broadcasted_iota(jnp.int32, (slots, slot_ref.shape[1]), 0)
    chosen = jnp.where(slot_ref[0:1, :] == spots, values, 0.0)
    return jnp.sum(chosen, axis=1, keepdims=True)


def hidden_kernel(given, count, first, last, where_ref, *refs):
    blocks, refs = refs[:given], refs[given:]
    wg, wu, refs = refs[0], refs[1 : 1 + count], refs[1 + count :]
    if not first:
        g_in, u_in, refs = refs[0], refs[1], refs[2:]
    if last:
        slot_ref, squares_ref, h_out, wide, inv = refs
    else:
        g_out, u_out, wide = refs
    n = pl.program_id(0)
    tile = wu[0].shape[1]

    @pl.when(n == 0)
    def _():
        place(where_ref, blocks, wide)
        if last:
            scale = 1.0 / jnp.sqrt(squares_ref[...] / D + epsilon)
            inv[...] = by_slot(slot_ref, scale, inv.shape[0])

    g = resident_product(where_ref, wide, wg, n, tile)
    u = product(wide, wu)
    at = pl.ds(pl.multiple_of(n * tile, 128), tile)
    if not first:
        g = g + g_in[:, at]
        u = u + u_in[:, at]
    if last:
        g = g * inv[...]
        u = u * inv[...]
        h_out[:, at] = (g / (1.0 + jnp.exp(-g)) * u).astype(BF)
    else:
        g_out[:, at] = g
        u_out[:, at] = u


def hidden_part(where, blocks, slots, w_gate, w_up, sums, rows_of):
    cols = blocks[0].shape[1]
    count = blocks[0].shape[0] // slots
    inner, width = w_up.shape
    tile, depth = 512 if slots > 272 else 1024, inner // 4
    first, last = sums is None, rows_of is not None
    w_gate = pltpu.with_memory_space_constraint(w_gate, pltpu.VMEM)
    w_up = pltpu.with_memory_space_constraint(w_up, pltpu.HBM)
    ins = [where, *blocks, w_gate] + [w_up] * count
    specs = whole_specs(blocks) + [VMEM] + weight_specs(count, depth, tile)
    aliases = {}
    if not first:
        if not last:
            aliases = {len(ins): 0, len(ins) + 1: 1}
        ins += [pltpu.with_memory_space_constraint(part, pltpu.VMEM) for part in sums]
        specs += [VMEM] * 2
    if last:
        ins += rows_of
        specs += whole_specs(rows_of)
        outs, out_specs = pltpu.VMEM((slots, width), BF), VMEM
    else:
        outs, out_specs = [pltpu.VMEM((slots, width), F32)] * 2, [VMEM] * 2
    return pl.pallas_call(
        functools.partial(hidden_kernel, len(blocks), count, first, last),
        out_shape=outs,
        grid_spec=pltpu.PrefetchScalarGridSpec(
            num_scalar_prefetch=1,
            grid=(width // tile,),
            in_specs=specs,
            out_specs=out_specs,
            scratch_shapes=[pltpu.VMEM((slots, 4 * count * cols), BF)]
            + [pltpu.VMEM((slots, 1), F32)] * last,
        ),
        input_output_aliases=aliases,
        compiler_params=params(30),
        cost_estimate=cost(slots, 8 if first else count * depth, 2 * width, 0),
    )(*ins)


def down_kernel(where_ref, h_ref, w_ref, slot_ref, row_ref, *refs):
    *outs, total, gate_ref = refs
    rows = h_ref.shape[0]
    step = pl.program_id(0)

    @pl.when(step == 0)
    def _():
        gate_ref[...] = by_slot(slot_ref, row_ref[...], rows)

    value = jnp.dot(h_ref[...], w_ref[...], preferred_element_type=F32) * gate_ref[...]
    total[...] = value
    for c in range(4):
        own, across, core = outs[3 * (c // 2) : 3 * (c // 2) + 3]
        g = c % 2

        @pl.when(step == c)
        def _():
            cols = own.shape[1]
            for b in range(4):
                part = total[:, pl.ds(pl.multiple_of(where_ref[b] * cols, 128), cols)]
                if b < 2:
                    (own, across)[b][g * rows : (g + 1) * rows, :] = part
                else:
                    first = ((b - 2) * 2 + g) * rows
                    core[first : first + rows, :] = part.astype(BF)


def down_all(where, hidden, w_down, slot_rows, gate_row, cols):
    rows, inner = hidden.shape
    hidden = pltpu.with_memory_space_constraint(hidden, pltpu.VMEM)
    sizes = ((2 * rows, F32), (2 * rows, F32), (4 * rows, BF)) * 2
    return pl.pallas_call(
        down_kernel,
        out_shape=[jax.ShapeDtypeStruct((count, cols), kind) for count, kind in sizes],
        grid_spec=pltpu.PrefetchScalarGridSpec(
            num_scalar_prefetch=1,
            grid=(4,),
            in_specs=[
                VMEM,
                pl.BlockSpec((inner, 4 * cols), lambda j, w: (0, w[4 + j])),
                *whole_specs([slot_rows, gate_row]),
            ],
            out_specs=[pl.BlockSpec((count, cols), lambda j, w: (0, 0)) for count, _ in sizes],
            scratch_shapes=[pltpu.VMEM((rows, 4 * cols), F32), pltpu.VMEM((rows, 1), F32)],
        ),
        compiler_params=params(40),
        cost_estimate=cost(rows, inner, 16 * cols, 64 * rows * cols),
    )(where, hidden, w_down, slot_rows, gate_row)


def mix_kernel(slot_ref, x_ref, gain_ref, e0, e2, e1, e3, out_ref, squares_ref):
    rows = x_ref.shape[0]
    mixture = x_ref[...].astype(F32)
    moe = jnp.zeros_like(mixture)
    for j, part in enumerate((e0, e1, e2, e3)):
        slots = part.shape[0]
        spots = lax.broadcasted_iota(jnp.int32, (rows, slots), 1)
        chosen = jnp.where(slot_ref[:, j : j + 1] == spots, 1.0, 0.0).astype(BF)
        moe = moe + jnp.dot(chosen, part[...], preferred_element_type=F32)
    mixture = mixture + moe
    out_ref[...] = (mixture * gain_ref[...].astype(F32)).astype(BF)
    squares_ref[...] = jnp.sum(mixture * mixture, axis=1, keepdims=True)


def mix(slot_cols, x, gain, parts):
    rows, cols = x.shape
    return pl.pallas_call(
        mix_kernel,
        out_shape=[
            jax.ShapeDtypeStruct((rows, cols), BF),
            jax.ShapeDtypeStruct((rows, 1), F32),
        ],
        compiler_params=params(16),
    )(slot_cols, x, gain, *parts)


def vocab_kernel(given, count, first, last, tile, where_ref, *refs):
    blocks, refs = refs[:given], refs[given:]
    weight, refs = refs[0], refs[1:]
    if not first:
        sum_in, refs = refs[0], refs[1:]
    if last:
        inv, local_ids, out, wide, top, total, picked = refs
    else:
        out, wide = refs
    n = pl.program_id(0)

    @pl.when(n == 0)
    def _():
        place(where_ref, blocks, wide)

    value = resident_product(where_ref, wide, weight, n, tile)
    at = pl.ds(pl.multiple_of(n * tile, 128), tile)
    if not first:
        value = value + sum_in[:, at]
    if not last:
        out[:, at] = value
        return
    logits = value * (1.0 / jnp.sqrt(inv[...] / D + epsilon))
    column = n * tile + lax.broadcasted_iota(jnp.int32, logits.shape, 1)
    tile_pick = jnp.sum(jnp.where(column == local_ids[...], logits, 0.0), axis=1, keepdims=True)
    tile_top = jnp.max(logits, axis=1, keepdims=True)

    @pl.when(n == 0)
    def _():
        top[...] = tile_top
        total[...] = jnp.sum(jnp.exp(logits - tile_top), axis=1, keepdims=True)
        picked[...] = tile_pick

    @pl.when(n > 0)
    def _():
        new_top = jnp.maximum(top[...], tile_top)
        total[...] = total[...] * jnp.exp(top[...] - new_top) + jnp.sum(
            jnp.exp(logits - new_top), axis=1, keepdims=True
        )
        top[...] = new_top
        picked[...] = picked[...] + tile_pick

    @pl.when(n == pl.num_programs(0) - 1)
    def _():
        lane = lax.broadcasted_iota(jnp.int32, out.shape, 1)
        out[...] = jnp.where(lane == 0, top[...], jnp.where(lane == 1, total[...], picked[...]))


def vocab_part(where, blocks, rows, lm_head, sums, inv, local_ids):
    cols = blocks[0].shape[1]
    count = blocks[0].shape[0] // rows
    inner, width = lm_head.shape
    tile = 512 if rows <= 352 else 256
    first, last = sums is None, inv is not None
    lm_head = pltpu.with_memory_space_constraint(lm_head, pltpu.VMEM)
    ins = [where, *blocks, lm_head]
    specs = whole_specs(blocks) + [VMEM]
    aliases = {}
    if not first:
        if not last:
            aliases = {len(ins): 0}
        ins.append(pltpu.with_memory_space_constraint(sums, pltpu.VMEM))
        specs.append(VMEM)
    scratch = [pltpu.VMEM((rows, 4 * count * cols), BF)]
    if last:
        ins += [inv, local_ids]
        specs += whole_specs([inv, local_ids])
        outs = jax.ShapeDtypeStruct((rows, 128), F32)
        out_specs = pl.BlockSpec((rows, 128), lambda n, w: (0, 0))
        scratch += [pltpu.VMEM((rows, 1), F32)] * 3
    else:
        outs, out_specs = pltpu.VMEM((rows, width), F32), VMEM
    return pl.pallas_call(
        functools.partial(vocab_kernel, len(blocks), count, first, last, tile),
        out_shape=outs,
        grid_spec=pltpu.PrefetchScalarGridSpec(
            num_scalar_prefetch=1,
            grid=(width // tile,),
            in_specs=specs,
            out_specs=out_specs,
            scratch_shapes=scratch,
        ),
        input_output_aliases=aliases,
        compiler_params=params(32),
        cost_estimate=cost(rows, 8 if first else inner * count // 4, width, 0),
    )(*ins)


def spread(by_offset, squares, load, part):
    own0 = by_offset[0]
    a1 = send(by_offset[1], plane_pairs(1))
    a3 = send(by_offset[3], plane_pairs(3))
    row0 = send(own0, xor_pairs(2))
    core0 = send(own0, xor_pairs(1))
    diagonal0 = send(own0, xor_pairs(3))
    weight, token = load(own0)

    near = jnp.concatenate([a1, a3], axis=0)
    row0, core0, diagonal0, near, squares, far, token = lax.optimization_barrier(
        (row0, core0, diagonal0, near, squares, by_offset[2], token)
    )
    a2 = send(far, plane_pairs(2))
    row13 = send(near, xor_pairs(2))
    squares = squares + token[:1, :1]
    more = [send(squares, xor_pairs(mask)) for mask in (1, 2, 3)]
    sums = part(0, weight, (own0, row0, core0, diagonal0), None, None)

    a2, row13, squares, more, sums = lax.optimization_barrier((a2, row13, squares, more, sums))
    row2 = send(a2, xor_pairs(2))
    core13 = send(jnp.concatenate([near, row13], axis=0), xor_pairs(1))
    squares = squares + more[0] + (more[1] + more[2])
    more = [send(squares, plane_pairs(k)) for k in (1, 2, 3)]
    sums = part(1, weight, (near, row13, core13), sums, None)

    row2, squares, more, sums = lax.optimization_barrier((row2, squares, more, sums))
    squares = squares + more[0] + (more[1] + more[2])
    core2 = send(jnp.concatenate([a2, row2], axis=0), xor_pairs(1))
    return part(2, weight, (a2, row2, core2), sums, squares)


def live_part(
    x,
    norm_gain,
    final_gain,
    w_gate,
    w_up,
    w_down,
    lm_head,
    target_ids,
    slot_rows,
    gate_row,
    in_squares,
    where,
    down_at,
    first_id,
    live_rows,
    slots,
):
    cols = x.shape[1]
    *picked_rows, x_live = dispatch(slot_rows, x, norm_gain, slots, live_rows)
    packed = slot_rows[4]
    live_at = packed[None, :] == jnp.arange(live_rows, dtype=jnp.int32)[:, None]
    slot_live = jnp.stack(
        [
            jnp.sum(jnp.where(live_at, slot_rows[(4 - k) % 4][None, :] + 1, 0), axis=1) - 1
            for k in range(4)
        ],
        axis=1,
    )
    local_ids = (
        jnp.sum(jnp.where(live_at, target_ids[None, :], 0), axis=1, keepdims=True) - first_id
    )

    def hidden_step(group, weight, blocks, sums, squares):
        rows_of = None if squares is None else [slot_rows, squares]
        return hidden_part(where[group], blocks, slots, weight, w_up, sums, rows_of)

    hidden = spread(
        picked_rows, in_squares, functools.partial(resident, w_gate), hidden_step
    )

    two = 2 * slots
    own_a, row_a, core_a, own_b, row_b, core_b = down_all(
        down_at, hidden, w_down, slot_rows, gate_row, cols
    )
    heard_a = send(core_a, xor_pairs(1))
    heard_b = send(core_b, xor_pairs(1))
    across_a = (row_a + heard_a[two:].astype(F32)).astype(BF)
    crossed_a = send(across_a, xor_pairs(2))
    total_a = (own_a + heard_a[:two].astype(F32) + crossed_a.astype(F32)).astype(BF)
    part2 = send(total_a[:slots], plane_pairs(2))
    part1 = send(total_a[slots:], plane_pairs(1))
    across_b = (row_b + heard_b[two:].astype(F32)).astype(BF)
    crossed_b = send(after(across_b, crossed_a), xor_pairs(2))
    total_b = (own_b + heard_b[:two].astype(F32) + crossed_b.astype(F32)).astype(BF)
    part3 = send(total_b[:slots], plane_pairs(3))
    parts = (total_b[slots:], part2, part1, part3)

    scaled, squares = mix(slot_live, x_live, final_gain, parts)

    def vocab_step(group, weight, blocks, sums, squares):
        return vocab_part(where[group], blocks, live_rows, weight, sums, squares, local_ids)

    stats = spread([scaled] * 4, squares, functools.partial(resident, lm_head), vocab_step)
    spot = packed[:, None] == jnp.arange(live_rows, dtype=jnp.int32)[None, :]
    return jnp.stack(
        [jnp.sum(jnp.where(spot, stats[:, j][None, :], 0.0), axis=1) for j in range(3)]
    )


def fast_body(
    residual_in,
    norm_gain,
    final_gain,
    expert_ids,
    gate_values,
    w_gate,
    w_up,
    w_down,
    lm_head,
    target_ids,
    lengths,
):
    tokens = residual_in.shape[0]
    devices = lax.axis_size("tensor")
    me = lax.axis_index("tensor").astype(jnp.int32)
    plane, row, core = me >> 2, (me >> 1) & 1, me & 1
    slot_rows, gate_row, need = route(plane, lengths, expert_ids.T, gate_values.T)
    need = jnp.maximum(need, lax.ppermute(need, "groups", [(0, 1), (1, 0)]))

    at = [row * 2 + core, (1 - row) * 2 + core, row * 2 + 1 - core, (1 - row) * 2 + 1 - core]
    planes = [(plane + k) & 3 for k in range(4)]
    where = [jnp.stack(at + [planes[(4 - k) % 4] for k in group]) for group in CHUNKS]
    down_at = jnp.stack(at + [planes[k] for k in (2, 1, 3, 0)])
    stream = residual_in.astype(F32)
    in_squares = jnp.sum(stream * stream, axis=1)[None, :]

    stats = lax.switch(
        need[0, 0].astype(jnp.int32),
        [
            functools.partial(live_part, live_rows=rows, slots=slots)
            for rows, slots in TIERS + ((tokens, CAP),)
        ],
        residual_in,
        norm_gain[None, :],
        final_gain[None, :],
        w_gate,
        w_up,
        w_down,
        lm_head,
        target_ids,
        slot_rows,
        gate_row,
        in_squares,
        where,
        down_at,
        me * lm_head.shape[1],
    )
    rows_dev = tokens // devices
    stats = stats.reshape(3, devices, rows_dev).transpose(1, 0, 2)
    stats = lax.all_to_all(stats, "tensor", 0, 0, tiled=True)
    top = jnp.max(stats[:, 0], axis=0)
    total = jnp.sum(stats[:, 1] * jnp.exp(stats[:, 0] - top[None, :]), axis=0)
    logprob = jnp.sum(stats[:, 2], axis=0) - top - jnp.log(total)
    own_live = lax.dynamic_slice_in_dim(slot_rows[4], me * rows_dev, rows_dev) >= 0
    return jnp.where(own_live, logprob, 0.0)


def body(*args):
    if lax.axis_size("tensor") == 16 and lax.axis_size("groups") == 2:
        return fast_body(*args)
    return plain_body(*args)


def solution(mesh):
    return jax.shard_map(
        body,
        mesh=mesh,
        in_specs=(
            P("groups", "tensor"),
            P("tensor"),
            P("tensor"),
            P("groups", None),
            P("groups", None),
            P(None, "tensor"),
            P(None, "tensor"),
            P("tensor", None),
            P(None, "tensor"),
            P("groups"),
            P("groups"),
        ),
        out_specs=P(("groups", "tensor")),
        check_vma=False,
    )
```

profile of v0, /device:TPU:0, one launch (start us, length us, event | category | flops | bytes accessed | tf_op | source)
XLA Modules:
  0.0 213.1 jit_solution(16236424586852649509)
XLA Ops:
  2.8 3.0 %collective-permute-start.117 = (f32[8,128]{1,0:T(8,128)S(1)}, f32[8,128]{1,0:T(8,128)S(1)}, u32[]{:S(2)}, u32[]{:S(2)}) collective-permute-start(f32[8,128]{1,0:T(8,128)S(1)} %get-tuple-element.349), channel_id=1, source_target_pairs={{0,16},{16,0},{1,17},{17,1},{2,18},{18,2},{3,19},{19,3},{4,20},{20... | collective-permute-start | bytes 12296 | tf_op jit(solution)/shard_map/ppermute | solution.py:674
  9.8 189.4 %conditional.1 = (f32[3,512]{1,0:T(4,128)S(1)}) conditional(s32[]{:T(128)} %bitcast.39, (s32[8,512]{1,0:T(8,128)S(1)}, bf16[512,384]{1,0:T(8,128)(2,1)}, bf16[1,384]{1,0:T(2,128)(2,1)S(1)}, bf16[6144,2048]{1,0:T(8,128)(2,1)}, f32[1,512]{1,0:T(1,128)S(1)}, /*index=5*/s32[5]{0:T(128)S(1)}, bf16[6144,2048]{1,0:T(8,128)(2,1)}, ...), branch_computations={%region_1.10_spmd, %region_10.19_spmd, %region_19.28_spmd} | conditional | flops 33885274112 | bytes 554224000 | solution.py:683
  18.6 1.9 branch_1_fun.11
  20.6 1.6 collective-permute-start.42
  22.2 2.2 %collective-permute-start.43 = (bf16[272,384]{1,0:T(8,128)(2,1)S(1)}, bf16[272,384]{1,0:T(8,128)(2,1)S(1)}, u32[]{:S(2)}, u32[]{:S(2)}) collective-permute-start(bf16[272,384]{1,0:T(8,128)(2,1)S(1)} %get-tuple-element.194), channel_id=1, source_target_pairs={{0,12},{1,13},{2,14},{3,15},{4,0},{5,1},{6,2},{7,3},{8,4},{9,5},{1... | collective-permute-start | bytes 626696 | tf_op jit(solution)/shard_map/cond/branch_1_fun/ppermute | solution.py:131
  26.6 8.2 %branch_1_fun.12 = (bf16[6144,2048]{1,0:T(8,128)(2,1)S(1)}, f32[8,128]{1,0:T(8,128)S(1)}) custom-call(bf16[6144,2048]{1,0:T(8,128)(2,1)} %get-tuple-element.197.w_ref, bf16[272,384]{1,0:T(8,128)(2,1)S(1)} %get-tuple-element.192.after_ref.refs_0_), custom_call_target="tpu_custom_call" | custom-call | bytes 50331648 | tf_op jit(solution)/shard_map/cond/branch_1_fun/pallas_call | solution.py:159
  34.9 1.6 collective-permute-start.45
  40.3 6.5 %branch_1_fun.13 = (f32[272,2048]{1,0:T(8,128)S(1)}, f32[272,2048]{1,0:T(8,128)S(1)}) custom-call(s32[5]{0:T(128)S(1)} %get-tuple-element.203.where_ref, bf16[272,384]{1,0:T(8,128)(2,1)} %copy-done.8, bf16[272,384]{1,0:T(8,128)(2,1)} %copy-done.67, bf16[272,384]{1,0:T(8,128)(2,1)} %copy-done.68, bf16[272,384]{1,0:T(8,128)(2,1)} %copy-done.69, ...), custom_call_target="tpu_custom_call" | custom-call | flops 17825792 | bytes 65536 | tf_op jit(solution)/shard_map/cond/branch_1_fun/pallas_call | solution.py:373
  49.1 2.6 %collective-permute-start.51 = (f32[1,512]{1,0:T(1,128)S(1)}, f32[1,512]{1,0:T(1,128)S(1)}, u32[]{:S(2)}, u32[]{:S(2)}) collective-permute-start(f32[1,512]{1,0:T(1,128)S(1)} %add_add_fusion.7), channel_id=1, source_target_pairs={{0,8},{1,9},{2,10},{3,11},{4,12},{5,13},{6,14},{7,15},{8,0},{9,1},... | collective-permute-start | bytes 6152 | tf_op jit(solution)/shard_map/cond/branch_1_fun/ppermute | solution.py:131
  54.0 11.3 %branch_1_fun.14 = (f32[272,2048]{1,0:T(8,128)S(1)}, f32[272,2048]{1,0:T(8,128)S(1)}) custom-call(s32[6]{0:T(128)S(1)} %get-tuple-element.216.where_ref, bf16[544,384]{1,0:T(8,128)(2,1)} %copy-done.17, bf16[544,384]{1,0:T(8,128)(2,1)} %copy-done.23, bf16[1088,384]{1,0:T(8,128)(2,1)} %copy-done.41, ...), custom_call_target="tpu_custom_call", output_to_operand_aliasing={{0}: (7, {}), {1}: (8, {})} | custom-call | flops 6845104128 | bytes 25165824 | tf_op jit(solution)/shard_map/cond/branch_1_fun/pallas_call | solution.py:373
  68.0 6.9 %branch_1_fun.15.h_ref = bf16[272,2048]{1,0:T(8,128)(2,1)S(1)} custom-call(s32[5]{0:T(128)S(1)} %get-tuple-element.186.where_ref, bf16[272,384]{1,0:T(8,128)(2,1)} %copy-done.42, bf16[272,384]{1,0:T(8,128)(2,1)} %copy-done.43, bf16[544,384]{1,0:T(8,128)(2,1)} %copy-done.51, bf16[6144,2048]{1,0:T(8,128)(2,1)S(1)} %get-tuple-element.207.refs_4_.refs_3_, ...), custom_call_target="tpu_custom_call" | custom-call | flops 3422552064 | bytes 12582912 | tf_op jit(solution)/shard_map/cond/branch_1_fun/pallas_call | solution.py:373
  74.9 12.6 %branch_1_fun.16 = (f32[544,384]{1,0:T(8,128)S(1)}, f32[544,384]{1,0:T(8,128)S(1)}, bf16[1088,384]{1,0:T(8,128)(2,1)S(1)}, f32[544,384]{1,0:T(8,128)S(1)}, f32[5...) custom-call(s32[8]{0:T(128)S(1)} %get-tuple-element.191.where_ref, bf16[272,2048]{1,0:T(8,128)(2,1)S(1)} %branch_1_fun.15.h_ref, ...), custom_call_target="tpu_custom_call" | custom-call | flops 6845104128 | bytes 31850496 | tf_op jit(solution)/shard_map/cond/branch_1_fun/pallas_call | solution.py:421
  90.1 1.6 collective-permute-start.57
  91.7 10.1 %collective-permute-done.57 = bf16[544,384]{1,0:T(8,128)(2,1)S(1)} collective-permute-done((bf16[544,384]{1,0:T(8,128)(2,1)S(1)}, bf16[544,384]{1,0:T(8,128)(2,1)S(1)}, u32[]{:S(2)}, u32[]{:S(2)}) %collective-permute-start.57) | collective-permute-done | bytes 417824 | tf_op jit(solution)/shard_map/cond/branch_1_fun/ppermute | solution.py:131
  101.8 1.5 collective-permute-start.58
  103.5 2.0 collective-permute-start.59
  105.5 7.1 %collective-permute-done.58 = bf16[544,384]{1,0:T(8,128)(2,1)S(1)} collective-permute-done((bf16[544,384]{1,0:T(8,128)(2,1)S(1)}, bf16[544,384]{1,0:T(8,128)(2,1)S(1)}, u32[]{:S(2)}, u32[]{:S(2)}) %collective-permute-start.58) | collective-permute-done | bytes 417824 | tf_op jit(solution)/shard_map/cond/branch_1_fun/ppermute | solution.py:131
  114.3 6.1 %collective-permute-done.59.e2 = bf16[272,384]{1,0:T(8,128)(2,1)S(1)} collective-permute-done((bf16[272,384]{1,0:T(8,128)(2,1)S(1)}, bf16[272,384]{1,0:T(8,128)(2,1)S(1)}, u32[]{:S(2)}, u32[]{:S(2)}) %collective-permute-start.59) | collective-permute-done | bytes 208928 | tf_op jit(solution)/shard_map/cond/branch_1_fun/ppermute | solution.py:131
  120.4 3.6 %collective-permute-done.61.e3 = bf16[272,384]{1,0:T(8,128)(2,1)S(1)} collective-permute-done((bf16[272,384]{1,0:T(8,128)(2,1)S(1)}, bf16[272,384]{1,0:T(8,128)(2,1)S(1)}, u32[]{:S(2)}, u32[]{:S(2)}) %collective-permute-start.61) | collective-permute-done | bytes 208928 | tf_op jit(solution)/shard_map/cond/branch_1_fun/ppermute | solution.py:131
  125.7 3.2 %collective-permute-start.66 = (bf16[352,384]{1,0:T(8,128)(2,1)S(1)}, bf16[352,384]{1,0:T(8,128)(2,1)S(1)}, u32[]{:S(2)}, u32[]{:S(2)}) collective-permute-start(bf16[352,384]{1,0:T(8,128)(2,1)S(1)} %get-tuple-element.242.after_ref.refs_0_), channel_id=1, source_target_pairs={{0,12},{1,13},{2,14},{3,15},{4,0},{5,1},{6,2},{7,3},{8,4},{9,5},{1... | collective-permute-start | bytes 811016 | tf_op jit(solution)/shard_map/cond/branch_1_fun/ppermute | solution.py:131
  129.4 1.6 collective-permute-start.64
  131.0 8.2 %branch_1_fun.18 = (bf16[6144,2048]{1,0:T(8,128)(2,1)S(1)}, f32[8,128]{1,0:T(8,128)S(1)}) custom-call(bf16[6144,2048]{1,0:T(8,128)(2,1)} %get-tuple-element.240.w_ref, bf16[352,384]{1,0:T(8,128)(2,1)S(1)} %get-tuple-element.242.after_ref.refs_0_), custom_call_target="tpu_custom_call" | custom-call | bytes 50331648 | tf_op jit(solution)/shard_map/cond/branch_1_fun/pallas_call | solution.py:159
  143.7 1.5 collective-permute-start.70
  145.4 4.8 %branch_1_fun.19.refs_4_ = f32[352,2048]{1,0:T(8,128)S(1)} custom-call(s32[5]{0:T(128)S(1)} %get-tuple-element.203.where_ref, bf16[352,384]{1,0:T(8,128)(2,1)} %copy-done.6, bf16[352,384]{1,0:T(8,128)(2,1)} %copy-done.59, bf16[352,384]{1,0:T(8,128)(2,1)} %copy-done.60, bf16[352,384]{1,0:T(8,128)(2,1)} %copy-done.61, ...), custom_call_target="tpu_custom_call" | custom-call | flops 11534336 | bytes 32768 | tf_op jit(solution)/shard_map/cond/branch_1_fun/pallas_call | solution.py:538
  150.2 9.4 %collective-permute-done.70 = f32[352,1]{1,0:T(8,128)S(1)} collective-permute-done((f32[352,1]{1,0:T(8,128)S(1)}, f32[352,1]{1,0:T(8,128)S(1)}, u32[]{:S(2)}, u32[]{:S(2)}) %collective-permute-start.70) | collective-permute-done | bytes 1440 | tf_op jit(solution)/shard_map/cond/branch_1_fun/ppermute | solution.py:131
  159.6 4.2 %collective-permute-done.71 = f32[352,1]{1,0:T(8,128)S(1)} collective-permute-done((f32[352,1]{1,0:T(8,128)S(1)}, f32[352,1]{1,0:T(8,128)S(1)}, u32[]{:S(2)}, u32[]{:S(2)}) %collective-permute-start.71) | collective-permute-done | bytes 1440 | tf_op jit(solution)/shard_map/cond/branch_1_fun/ppermute | solution.py:131
  165.3 2.7 %collective-permute-start.75 = (f32[352,1]{1,0:T(8,128)S(1)}, f32[352,1]{1,0:T(8,128)S(1)}, u32[]{:S(2)}, u32[]{:S(2)}) collective-permute-start(f32[352,1]{1,0:T(8,128)S(1)} %add_add_fusion.5), channel_id=1, source_target_pairs={{0,12},{1,13},{2,14},{3,15},{4,0},{5,1},{6,2},{7,3},{8,4},{9,5},{1... | collective-permute-start | bytes 4232 | tf_op jit(solution)/shard_map/cond/branch_1_fun/ppermute | solution.py:131
  169.8 7.6 %branch_1_fun.20.refs_4_ = f32[352,2048]{1,0:T(8,128)S(1)} custom-call(s32[6]{0:T(128)S(1)} %get-tuple-element.216.where_ref, bf16[704,384]{1,0:T(8,128)(2,1)} %copy-done.15, bf16[704,384]{1,0:T(8,128)(2,1)} %copy-done.21, bf16[1408,384]{1,0:T(8,128)(2,1)} %copy-done.33, ...), custom_call_target="tpu_custom_call", output_to_operand_aliasing={{}: (5, {})} | custom-call | flops 4429185024 | bytes 12582912 | tf_op jit(solution)/shard_map/cond/branch_1_fun/pallas_call | solution.py:538
  177.5 2.8 %collective-permute-done.74 = f32[352,1]{1,0:T(8,128)S(1)} collective-permute-done((f32[352,1]{1,0:T(8,128)S(1)}, f32[352,1]{1,0:T(8,128)S(1)}, u32[]{:S(2)}, u32[]{:S(2)}) %collective-permute-start.74) | collective-permute-done | bytes 1440 | tf_op jit(solution)/shard_map/cond/branch_1_fun/ppermute | solution.py:131
  183.2 7.3 %branch_1_fun.21 = f32[352,128]{1,0:T(8,128)} custom-call(s32[5]{0:T(128)S(1)} %get-tuple-element.186.where_ref, bf16[352,384]{1,0:T(8,128)(2,1)} %copy-done.31, bf16[352,384]{1,0:T(8,128)(2,1)} %copy-done.32, bf16[704,384]{1,0:T(8,128)(2,1)} %copy-done.49, bf16[6144,2048]{1,0:T(8,128)(2,1)S(1)} %get-tuple-element.249.refs_4_.refs_3_, ...), custom_call_target="tpu_custom_call" | custom-call | flops 2214592512 | bytes 6291456 | tf_op jit(solution)/shard_map/cond/branch_1_fun/pallas_call | solution.py:538
  200.0 5.6 %all-to-all-start = ((f32[16,3,32]{2,1,0:T(4,128)}), f32[16,3,32]{2,1,0:T(4,128)S(1)}, u32[]{:S(2)}, u32[]{:S(2)}) async-start(f32[16,3,32]{2,1,0:T(4,128)} %copy.57), calls=%async_computation | async-start | bytes 65536 | tf_op jit(solution)/shard_map/all_to_all | solution.py:706
  205.5 6.6 %all-to-all-done = f32[16,3,32]{2,1,0:T(4,128)S(1)} async-done(((f32[16,3,32]{2,1,0:T(4,128)}), f32[16,3,32]{2,1,0:T(4,128)S(1)}, u32[]{:S(2)}, u32[]{:S(2)}) %all-to-all-start) | async-done | bytes 6176 | tf_op jit(solution)/shard_map/all_to_all | solution.py:706
  (162 shorter events, 39.5 us)
Async XLA Ops:
  20.6 14.2 %collective-permute-start.42 = (bf16[272,384]{1,0:T(8,128)(2,1)S(1)}, bf16[272,384]{1,0:T(8,128)(2,1)S(1)}, u32[]{:S(2)}, u32[]{:S(2)}) collective-permute-start(bf16[272,384]{1,0:T(8,128)(2,1)S(1)} %get-tuple-element.193), channel_id=1, source_target_pairs={{0,4},{1,5},{2,6},{3,7},{4,8},{5,9},{6,10},{7,11},{8,12},{9,13},{1... | collective-permute-start | bytes 626696 | tf_op jit(solution)/shard_map/cond/branch_1_fun/ppermute | solution.py:131
  22.2 12.6 %collective-permute-start.43 = (bf16[272,384]{1,0:T(8,128)(2,1)S(1)}, bf16[272,384]{1,0:T(8,128)(2,1)S(1)}, u32[]{:S(2)}, u32[]{:S(2)}) collective-permute-start(bf16[272,384]{1,0:T(8,128)(2,1)S(1)} %get-tuple-element.194), channel_id=1, source_target_pairs={{0,12},{1,13},{2,14},{3,15},{4,0},{5,1},{6,2},{7,3},{8,4},{9,5},{1... | collective-permute-start | bytes 626696 | tf_op jit(solution)/shard_map/cond/branch_1_fun/ppermute | solution.py:131
  24.5 10.4 %collective-permute-start.39 = (bf16[272,384]{1,0:T(8,128)(2,1)S(1)}, bf16[272,384]{1,0:T(8,128)(2,1)S(1)}, u32[]{:S(2)}, u32[]{:S(2)}) collective-permute-start(bf16[272,384]{1,0:T(8,128)(2,1)S(1)} %get-tuple-element.192.after_ref.refs_0_), channel_id=1, source_target_pairs={{0,2},{1,3},{2,0},{3,1},{4,6},{5,7},{6,4},{7,5},{8,10},{9,11},{10,... | collective-permute-start | bytes 626696 | tf_op jit(solution)/shard_map/cond/branch_1_fun/ppermute | solution.py:131
  26.0 8.9 %collective-permute-start.40 = (bf16[272,384]{1,0:T(8,128)(2,1)S(1)}, bf16[272,384]{1,0:T(8,128)(2,1)S(1)}, u32[]{:S(2)}, u32[]{:S(2)}) collective-permute-start(bf16[272,384]{1,0:T(8,128)(2,1)S(1)} %get-tuple-element.192.after_ref.refs_0_), channel_id=1, source_target_pairs={{0,1},{1,0},{2,3},{3,2},{4,5},{5,4},{6,7},{7,6},{8,9},{9,8},{10,11... | collective-permute-start | bytes 626696 | tf_op jit(solution)/shard_map/cond/branch_1_fun/ppermute | solution.py:131
  26.0 8.9 %collective-permute-start.41 = (bf16[272,384]{1,0:T(8,128)(2,1)S(1)}, bf16[272,384]{1,0:T(8,128)(2,1)S(1)}, u32[]{:S(2)}, u32[]{:S(2)}) collective-permute-start(bf16[272,384]{1,0:T(8,128)(2,1)S(1)} %get-tuple-element.192.after_ref.refs_0_), channel_id=1, source_target_pairs={{0,3},{1,2},{2,1},{3,0},{4,7},{5,6},{6,5},{7,4},{8,11},{9,10},{10,... | collective-permute-start | bytes 626696 | tf_op jit(solution)/shard_map/cond/branch_1_fun/ppermute | solution.py:131
  34.9 13.5 %collective-permute-start.45 = (bf16[544,384]{1,0:T(8,128)(2,1)S(1)}, bf16[544,384]{1,0:T(8,128)(2,1)S(1)}, u32[]{:S(2)}, u32[]{:S(2)}) collective-permute-start(bf16[544,384]{1,0:T(8,128)(2,1)S(1)} %pad_maximum_fusion.11.refs_0_), channel_id=1, source_target_pairs={{0,2},{1,3},{2,0},{3,1},{4,6},{5,7},{6,4},{7,5},{8,10},{9,11},{10,... | collective-permute-start | bytes 1253384 | tf_op jit(solution)/shard_map/cond/branch_1_fun/ppermute | solution.py:131
  37.0 11.4 %collective-permute-start.44 = (bf16[272,384]{1,0:T(8,128)(2,1)S(1)}, bf16[272,384]{1,0:T(8,128)(2,1)S(1)}, u32[]{:S(2)}, u32[]{:S(2)}) collective-permute-start(bf16[272,384]{1,0:T(8,128)(2,1)S(1)} %get-tuple-element.199), channel_id=1, source_target_pairs={{0,8},{1,9},{2,10},{3,11},{4,12},{5,13},{6,14},{7,15},{8,0},{9,1},... | collective-permute-start | bytes 626696 | tf_op jit(solution)/shard_map/cond/branch_1_fun/ppermute | solution.py:131
  38.4 8.5 %collective-permute-start.46 = (f32[1,512]{1,0:T(1,128)S(1)}, f32[1,512]{1,0:T(1,128)S(1)}, u32[]{:S(2)}, u32[]{:S(2)}) collective-permute-start(f32[1,512]{1,0:T(1,128)S(1)} %broadcast_add_fusion.7), channel_id=1, source_target_pairs={{0,1},{1,0},{2,3},{3,2},{4,5},{5,4},{6,7},{7,6},{8,9},{9,8},{10,11... | collective-permute-start | bytes 6152 | tf_op jit(solution)/shard_map/cond/branch_1_fun/ppermute | solution.py:131
  38.5 8.4 %collective-permute-start.47 = (f32[1,512]{1,0:T(1,128)S(1)}, f32[1,512]{1,0:T(1,128)S(1)}, u32[]{:S(2)}, u32[]{:S(2)}) collective-permute-start(f32[1,512]{1,0:T(1,128)S(1)} %broadcast_add_fusion.7), channel_id=1, source_target_pairs={{0,2},{1,3},{2,0},{3,1},{4,6},{5,7},{6,4},{7,5},{8,10},{9,11},{10,... | collective-permute-start | bytes 6152 | tf_op jit(solution)/shard_map/cond/branch_1_fun/ppermute | solution.py:131
  48.6 16.7 %collective-permute-start.50 = (f32[1,512]{1,0:T(1,128)S(1)}, f32[1,512]{1,0:T(1,128)S(1)}, u32[]{:S(2)}, u32[]{:S(2)}) collective-permute-start(f32[1,512]{1,0:T(1,128)S(1)} %add_add_fusion.7), channel_id=1, source_target_pairs={{0,4},{1,5},{2,6},{3,7},{4,8},{5,9},{6,10},{7,11},{8,12},{9,13},{1... | collective-permute-start | bytes 6152 | tf_op jit(solution)/shard_map/cond/branch_1_fun/ppermute | solution.py:131
  49.1 16.2 %collective-permute-start.51 = (f32[1,512]{1,0:T(1,128)S(1)}, f32[1,512]{1,0:T(1,128)S(1)}, u32[]{:S(2)}, u32[]{:S(2)}) collective-permute-start(f32[1,512]{1,0:T(1,128)S(1)} %add_add_fusion.7), channel_id=1, source_target_pairs={{0,8},{1,9},{2,10},{3,11},{4,12},{5,13},{6,14},{7,15},{8,0},{9,1},... | collective-permute-start | bytes 6152 | tf_op jit(solution)/shard_map/cond/branch_1_fun/ppermute | solution.py:131
  51.7 13.6 %collective-permute-start.52 = (f32[1,512]{1,0:T(1,128)S(1)}, f32[1,512]{1,0:T(1,128)S(1)}, u32[]{:S(2)}, u32[]{:S(2)}) collective-permute-start(f32[1,512]{1,0:T(1,128)S(1)} %add_add_fusion.7), channel_id=1, source_target_pairs={{0,12},{1,13},{2,14},{3,15},{4,0},{5,1},{6,2},{7,3},{8,4},{9,5},{1... | collective-permute-start | bytes 6152 | tf_op jit(solution)/shard_map/cond/branch_1_fun/ppermute | solution.py:131
  52.5 12.8 %collective-permute-start.49 = (bf16[272,384]{1,0:T(8,128)(2,1)S(1)}, bf16[272,384]{1,0:T(8,128)(2,1)S(1)}, u32[]{:S(2)}, u32[]{:S(2)}) collective-permute-start(bf16[272,384]{1,0:T(8,128)(2,1)S(1)} %collective-permute-done.44.refs_0_), channel_id=1, source_target_pairs={{0,2},{1,3},{2,0},{3,1},{4,6},{5,7},{6,4},{7,5},{8,10},{9,11},{10,... | collective-permute-start | bytes 626696 | tf_op jit(solution)/shard_map/cond/branch_1_fun/ppermute | solution.py:131
  90.1 11.8 %collective-permute-start.57 = (bf16[544,384]{1,0:T(8,128)(2,1)S(1)}, bf16[544,384]{1,0:T(8,128)(2,1)S(1)}, u32[]{:S(2)}, u32[]{:S(2)}) collective-permute-start(bf16[544,384]{1,0:T(8,128)(2,1)S(1)} %add_convert_fusion.6), channel_id=1, source_target_pairs={{0,2},{1,3},{2,0},{3,1},{4,6},{5,7},{6,4},{7,5},{8,10},{9,11},{10,... | collective-permute-start | bytes 1253384 | tf_op jit(solution)/shard_map/cond/branch_1_fun/ppermute | solution.py:131
  101.8 10.9 %collective-permute-start.58 = (bf16[544,384]{1,0:T(8,128)(2,1)S(1)}, bf16[544,384]{1,0:T(8,128)(2,1)S(1)}, u32[]{:S(2)}, u32[]{:S(2)}) collective-permute-start(bf16[544,384]{1,0:T(8,128)(2,1)S(1)} %add_convert_fusion.7), channel_id=1, source_target_pairs={{0,2},{1,3},{2,0},{3,1},{4,6},{5,7},{6,4},{7,5},{8,10},{9,11},{10,... | collective-permute-start | bytes 1253384 | tf_op jit(solution)/shard_map/cond/branch_1_fun/ppermute | solution.py:131
  103.5 16.9 %collective-permute-start.59 = (bf16[272,384]{1,0:T(8,128)(2,1)S(1)}, bf16[272,384]{1,0:T(8,128)(2,1)S(1)}, u32[]{:S(2)}, u32[]{:S(2)}) collective-permute-start(bf16[272,384]{1,0:T(8,128)(2,1)S(1)} %get-tuple-element.400), channel_id=1, source_target_pairs={{0,8},{1,9},{2,10},{3,11},{4,12},{5,13},{6,14},{7,15},{8,0},{9,1},... | collective-permute-start | bytes 626696 | tf_op jit(solution)/shard_map/cond/branch_1_fun/ppermute | solution.py:131
  105.5 14.9 %collective-permute-start.60 = (bf16[272,384]{1,0:T(8,128)(2,1)S(1)}, bf16[272,384]{1,0:T(8,128)(2,1)S(1)}, u32[]{:S(2)}, u32[]{:S(2)}) collective-permute-start(bf16[272,384]{1,0:T(8,128)(2,1)S(1)} %get-tuple-element.399), channel_id=1, source_target_pairs={{0,4},{1,5},{2,6},{3,7},{4,8},{5,9},{6,10},{7,11},{8,12},{9,13},{1... | collective-permute-start | bytes 626696 | tf_op jit(solution)/shard_map/cond/branch_1_fun/ppermute | solution.py:131
  112.9 11.1 %collective-permute-start.61 = (bf16[272,384]{1,0:T(8,128)(2,1)S(1)}, bf16[272,384]{1,0:T(8,128)(2,1)S(1)}, u32[]{:S(2)}, u32[]{:S(2)}) collective-permute-start(bf16[272,384]{1,0:T(8,128)(2,1)S(1)} %get-tuple-element.397), channel_id=1, source_target_pairs={{0,12},{1,13},{2,14},{3,15},{4,0},{5,1},{6,2},{7,3},{8,4},{9,5},{1... | collective-permute-start | bytes 626696 | tf_op jit(solution)/shard_map/cond/branch_1_fun/ppermute | solution.py:131
  125.0 14.2 %collective-permute-start.65 = (bf16[352,384]{1,0:T(8,128)(2,1)S(1)}, bf16[352,384]{1,0:T(8,128)(2,1)S(1)}, u32[]{:S(2)}, u32[]{:S(2)}) collective-permute-start(bf16[352,384]{1,0:T(8,128)(2,1)S(1)} %get-tuple-element.242.after_ref.refs_0_), channel_id=1, source_target_pairs={{0,4},{1,5},{2,6},{3,7},{4,8},{5,9},{6,10},{7,11},{8,12},{9,13},{1... | collective-permute-start | bytes 811016 | tf_op jit(solution)/shard_map/cond/branch_1_fun/ppermute | solution.py:131
  125.7 13.7 %collective-permute-start.66 = (bf16[352,384]{1,0:T(8,128)(2,1)S(1)}, bf16[352,384]{1,0:T(8,128)(2,1)S(1)}, u32[]{:S(2)}, u32[]{:S(2)}) collective-permute-start(bf16[352,384]{1,0:T(8,128)(2,1)S(1)} %get-tuple-element.242.after_ref.refs_0_), channel_id=1, source_target_pairs={{0,12},{1,13},{2,14},{3,15},{4,0},{5,1},{6,2},{7,3},{8,4},{9,5},{1... | collective-permute-start | bytes 811016 | tf_op jit(solution)/shard_map/cond/branch_1_fun/ppermute | solution.py:131
  128.9 10.5 %collective-permute-start.62 = (bf16[352,384]{1,0:T(8,128)(2,1)S(1)}, bf16[352,384]{1,0:T(8,128)(2,1)S(1)}, u32[]{:S(2)}, u32[]{:S(2)}) collective-permute-start(bf16[352,384]{1,0:T(8,128)(2,1)S(1)} %get-tuple-element.242.after_ref.refs_0_), channel_id=1, source_target_pairs={{0,2},{1,3},{2,0},{3,1},{4,6},{5,7},{6,4},{7,5},{8,10},{9,11},{10,... | collective-permute-start | bytes 811016 | tf_op jit(solution)/shard_map/cond/branch_1_fun/ppermute | solution.py:131
  129.4 10.0 %collective-permute-start.63 = (bf16[352,384]{1,0:T(8,128)(2,1)S(1)}, bf16[352,384]{1,0:T(8,128)(2,1)S(1)}, u32[]{:S(2)}, u32[]{:S(2)}) collective-permute-start(bf16[352,384]{1,0:T(8,128)(2,1)S(1)} %get-tuple-element.242.after_ref.refs_0_), channel_id=1, source_target_pairs={{0,1},{1,0},{2,3},{3,2},{4,5},{5,4},{6,7},{7,6},{8,9},{9,8},{10,11... | collective-permute-start | bytes 811016 | tf_op jit(solution)/shard_map/cond/branch_1_fun/ppermute | solution.py:131
  129.4 11.5 %collective-permute-start.64 = (bf16[352,384]{1,0:T(8,128)(2,1)S(1)}, bf16[352,384]{1,0:T(8,128)(2,1)S(1)}, u32[]{:S(2)}, u32[]{:S(2)}) collective-permute-start(bf16[352,384]{1,0:T(8,128)(2,1)S(1)} %get-tuple-element.242.after_ref.refs_0_), channel_id=1, source_target_pairs={{0,3},{1,2},{2,1},{3,0},{4,7},{5,6},{6,5},{7,4},{8,11},{9,10},{10,... | collective-permute-start | bytes 811016 | tf_op jit(solution)/shard_map/cond/branch_1_fun/ppermute | solution.py:131
  141.0 22.9 %collective-permute-start.68 = (bf16[704,384]{1,0:T(8,128)(2,1)S(1)}, bf16[704,384]{1,0:T(8,128)(2,1)S(1)}, u32[]{:S(2)}, u32[]{:S(2)}) collective-permute-start(bf16[704,384]{1,0:T(8,128)(2,1)S(1)} %pad_maximum_fusion.9.refs_0_), channel_id=1, source_target_pairs={{0,2},{1,3},{2,0},{3,1},{4,6},{5,7},{6,4},{7,5},{8,10},{9,11},{10,... | collective-permute-start | bytes 1622024 | tf_op jit(solution)/shard_map/cond/branch_1_fun/ppermute | solution.py:131
  142.1 21.7 %collective-permute-start.67 = (bf16[352,384]{1,0:T(8,128)(2,1)S(1)}, bf16[352,384]{1,0:T(8,128)(2,1)S(1)}, u32[]{:S(2)}, u32[]{:S(2)}) collective-permute-start(bf16[352,384]{1,0:T(8,128)(2,1)S(1)} %get-tuple-element.242.after_ref.refs_0_), channel_id=1, source_target_pairs={{0,8},{1,9},{2,10},{3,11},{4,12},{5,13},{6,14},{7,15},{8,0},{9,1},... | collective-permute-start | bytes 811016 | tf_op jit(solution)/shard_map/cond/branch_1_fun/ppermute | solution.py:131
  143.7 15.9 %collective-permute-start.70 = (f32[352,1]{1,0:T(8,128)S(1)}, f32[352,1]{1,0:T(8,128)S(1)}, u32[]{:S(2)}, u32[]{:S(2)}) collective-permute-start(f32[352,1]{1,0:T(8,128)S(1)} %broadcast_add_fusion.6), channel_id=1, source_target_pairs={{0,2},{1,3},{2,0},{3,1},{4,6},{5,7},{6,4},{7,5},{8,10},{9,11},{10,... | collective-permute-start | bytes 4232 | tf_op jit(solution)/shard_map/cond/branch_1_fun/ppermute | solution.py:131
  145.2 18.6 %collective-permute-start.71 = (f32[352,1]{1,0:T(8,128)S(1)}, f32[352,1]{1,0:T(8,128)S(1)}, u32[]{:S(2)}, u32[]{:S(2)}) collective-permute-start(f32[352,1]{1,0:T(8,128)S(1)} %broadcast_add_fusion.6), channel_id=1, source_target_pairs={{0,3},{1,2},{2,1},{3,0},{4,7},{5,6},{6,5},{7,4},{8,11},{9,10},{10,... | collective-permute-start | bytes 4232 | tf_op jit(solution)/shard_map/cond/branch_1_fun/ppermute | solution.py:131
  164.1 13.3 %collective-permute-start.73 = (f32[352,1]{1,0:T(8,128)S(1)}, f32[352,1]{1,0:T(8,128)S(1)}, u32[]{:S(2)}, u32[]{:S(2)}) collective-permute-start(f32[352,1]{1,0:T(8,128)S(1)} %add_add_fusion.5), channel_id=1, source_target_pairs={{0,4},{1,5},{2,6},{3,7},{4,8},{5,9},{6,10},{7,11},{8,12},{9,13},{1... | collective-permute-start | bytes 4232 | tf_op jit(solution)/shard_map/cond/branch_1_fun/ppermute | solution.py:131
  164.2 16.1 %collective-permute-start.74 = (f32[352,1]{1,0:T(8,128)S(1)}, f32[352,1]{1,0:T(8,128)S(1)}, u32[]{:S(2)}, u32[]{:S(2)}) collective-permute-start(f32[352,1]{1,0:T(8,128)S(1)} %add_add_fusion.5), channel_id=1, source_target_pairs={{0,8},{1,9},{2,10},{3,11},{4,12},{5,13},{6,14},{7,15},{8,0},{9,1},... | collective-permute-start | bytes 4232 | tf_op jit(solution)/shard_map/cond/branch_1_fun/ppermute | solution.py:131
  165.3 14.9 %collective-permute-start.75 = (f32[352,1]{1,0:T(8,128)S(1)}, f32[352,1]{1,0:T(8,128)S(1)}, u32[]{:S(2)}, u32[]{:S(2)}) collective-permute-start(f32[352,1]{1,0:T(8,128)S(1)} %add_add_fusion.5), channel_id=1, source_target_pairs={{0,12},{1,13},{2,14},{3,15},{4,0},{5,1},{6,2},{7,3},{8,4},{9,5},{1... | collective-permute-start | bytes 4232 | tf_op jit(solution)/shard_map/cond/branch_1_fun/ppermute | solution.py:131
  168.0 12.3 %collective-permute-start.72 = (bf16[352,384]{1,0:T(8,128)(2,1)S(1)}, bf16[352,384]{1,0:T(8,128)(2,1)S(1)}, u32[]{:S(2)}, u32[]{:S(2)}) collective-permute-start(bf16[352,384]{1,0:T(8,128)(2,1)S(1)} %collective-permute-done.67.refs_0_), channel_id=1, source_target_pairs={{0,2},{1,3},{2,0},{3,1},{4,6},{5,7},{6,4},{7,5},{8,10},{9,11},{10,... | collective-permute-start | bytes 811016 | tf_op jit(solution)/shard_map/cond/branch_1_fun/ppermute | solution.py:131
  200.0 12.2 %all-to-all-start = ((f32[16,3,32]{2,1,0:T(4,128)}), f32[16,3,32]{2,1,0:T(4,128)S(1)}, u32[]{:S(2)}, u32[]{:S(2)}) async-start(f32[16,3,32]{2,1,0:T(4,128)} %copy.57), calls=%async_computation | async-start | bytes 65536 | tf_op jit(solution)/shard_map/all_to_all | solution.py:706
  (33 other events, 207.6 us)
where the time goes:
time: 217 us; the launch traced here: 213 us
  Pallas kernels  77.1 us (36%)
  waiting for transfers between devices  56 us (26%)
  starting transfers between devices  44.6 us (21%)
  loops' own time  16.5 us (8%)
  local copies, waits for them, and re-layouts  11.9 us (5%)
  other arithmetic  5.92 us (3%)
    ppermute x39, waiting for transfers between devices, send(): return lax.ppermute(array, 'tensor', pairs)  49.4 us
    ppermute x39, starting transfers between devices, send(): return lax.ppermute(array, 'tensor', pairs)  36.1 us
    pallas_call x3, Pallas kernels, hidden_part(): pl.pallas_call(functools.partial(hidden_kernel, len(blocks), count, first...  24.8 us
    pallas_call x3, Pallas kernels, vocab_part(): pl.pallas_call(functools.partial(vocab_kernel, len(blocks), count, first,...  19.7 us
    another operation x1, loops' own time, fast_body(): lax.switch(need[0, 0].astype(jnp.int32), [functools.partial(live_part, li...  16.5 us
    pallas_call x2, Pallas kernels, resident(): pl.pallas_call(load_kernel, in_specs=[pl.BlockSpec(memory_space=pltpu.HBM...  16.3 us
    pallas_call x1, Pallas kernels, down_all(): pl.pallas_call(down_kernel, out_shape=[jax.ShapeDtypeStruct((count, cols)...  12.6 us
    all_to_all x1, waiting for transfers between devices, fast_body(): stats = lax.all_to_all(stats, 'tensor', 0, 0, tiled=True)  6.62 us
  transfers between devices with their start and end apart: 41, of which 14 were waited for; matrix products, arithmetic and copies ran while one was open for 4% of the time, Pallas kernels for 22%

commit v1 on v0

--- a/solution.py
+++ b/solution.py
@@ -120,7 +120,7 @@
     in_length = position % SEQ < lengths[position // SEQ]
     return jnp.where(in_length, own_rows, jnp.zeros_like(own_rows)).astype(jnp.float32)
 
-TIERS = ((288, 224), (352, 272))
+TIERS = ((304, 240), (352, 272))
 CHUNKS = ((0,), (1, 3), (2,))
 VMEM = pl.BlockSpec(memory_space=pltpu.VMEM)
 BF = jnp.bfloat16
@@ -485,7 +485,12 @@
     if not last:
         out[:, at] = value
         return
-    logits = value * (1.0 / jnp.sqrt(inv[...] / D + epsilon))
+    rows = value.shape[0]
+    same = lax.broadcasted_iota(jnp.int32, (rows, rows), 0) == lax.broadcasted_iota(
+        jnp.int32, (rows, rows), 1
+    )
+    squares = jnp.sum(jnp.where(same, inv[...], 0.0), axis=1, keepdims=True)
+    logits = value * (1.0 / jnp.sqrt(squares / D + epsilon))
     column = n * tile + lax.broadcasted_iota(jnp.int32, logits.shape, 1)
     tile_pick = jnp.sum(jnp.where(column == local_ids[...], logits, 0.0), axis=1, keepdims=True)
     tile_top = jnp.max(logits, axis=1, keepdims=True)
@@ -646,7 +651,8 @@
     def vocab_step(group, weight, blocks, sums, squares):
         return vocab_part(where[group], blocks, live_rows, weight, sums, squares, local_ids)
 
-    stats = spread([scaled] * 4, squares, functools.partial(resident, lm_head), vocab_step)
+    squares = squares.reshape(1, -1)
+    stats = spread([scaled] * 4, squares, lambda own: resident(lm_head, squares), vocab_step)
     spot = packed[:, None] == jnp.arange(live_rows, dtype=jnp.int32)[None, :]
     return jnp.stack(
         [jnp.sum(jnp.where(spot, stats[:, j][None, :], 0.0), axis=1) for j in range(3)]

time: 217 us -> 176 us (0.81); the launches traced: 213 us -> 175 us
  waiting for transfers between devices: 56 us -> 39.2 us
  loops' own time: 16.5 us -> 1.18 us
  Pallas kernels: 77.1 us -> 73 us
    ppermute x39, waiting for transfers between devices: 49.4 us -> 32.6 us  [send(): return lax.ppermute(array, 'tensor', pairs)]
    another operation x1, loops' own time: 16.5 us -> 1.18 us  [fast_body(): lax.switch(need[0, 0].astype(jnp.int32), [functools.partial(live_part, li...]
  transfers between devices with their start and end apart: 41 -> 41, of which waited for: 14 -> 11; matrix products, arithmetic and copies ran while one was open for 4% -> 5% of each run, Pallas kernels for 22% -> 25%
where the time goes in v1:
time: 176 us; the launch traced here: 175 us
  Pallas kernels  73 us (41%)
  starting transfers between devices  43 us (24%)
  waiting for transfers between devices  39.2 us (22%)
  local copies, waits for them, and re-layouts  11.9 us (7%)
  other arithmetic  5.99 us (3%)
    ppermute x39, starting transfers between devices, send(): return lax.ppermute(array, 'tensor', pairs)  36.3 us
    ppermute x39, waiting for transfers between devices, send(): return lax.ppermute(array, 'tensor', pairs)  32.6 us
    pallas_call x3, Pallas kernels, hidden_part(): pl.pallas_call(functools.partial(hidden_kernel, len(blocks), count, first...  23 us
    pallas_call x3, Pallas kernels, vocab_part(): pl.pallas_call(functools.partial(vocab_kernel, len(blocks), count, first,...  18.5 us
    pallas_call x2, Pallas kernels, resident(): pl.pallas_call(load_kernel, in_specs=[pl.BlockSpec(memory_space=pltpu.HBM...  16.3 us
    pallas_call x1, Pallas kernels, down_all(): pl.pallas_call(down_kernel, out_shape=[jax.ShapeDtypeStruct((count, cols)...  12 us
    all_to_all x1, waiting for transfers between devices, fast_body(): stats = lax.all_to_all(stats, 'tensor', 0, 0, tiled=True)  6.62 us
    all_to_all x1, starting transfers between devices, fast_body(): stats = lax.all_to_all(stats, 'tensor', 0, 0, tiled=True)  3.79 us
  transfers between devices with their start and end apart: 41, of which 11 were waited for; matrix products, arithmetic and copies ran while one was open for 5% of the time, Pallas kernels for 25%

profile of v1, /device:TPU:0, one launch (start us, length us, event | category | flops | bytes accessed | tf_op | source)
XLA Modules:
  0.0 175.0 jit_solution(8883884217003008837)
XLA Ops:
  2.8 3.0 %collective-permute-start.117 = (f32[8,128]{1,0:T(8,128)S(1)}, f32[8,128]{1,0:T(8,128)S(1)}, u32[]{:S(2)}, u32[]{:S(2)}) collective-permute-start(f32[8,128]{1,0:T(8,128)S(1)} %get-tuple-element.349), channel_id=1, source_target_pairs={{0,16},{16,0},{1,17},{17,1},{2,18},{18,2},{3,19},{19,3},{4,20},{20... | collective-permute-start | bytes 12296 | tf_op jit(solution)/shard_map/ppermute | solution.py:680
  9.8 153.4 %conditional.1 = (f32[3,512]{1,0:T(4,128)S(1)}) conditional(s32[]{:T(128)} %bitcast.39, (s32[8,512]{1,0:T(8,128)S(1)}, bf16[512,384]{1,0:T(8,128)(2,1)}, bf16[1,384]{1,0:T(2,128)(2,1)S(1)}, bf16[6144,2048]{1,0:T(8,128)(2,1)}, f32[1,512]{1,0:T(1,128)S(1)}, /*index=5*/s32[5]{0:T(128)S(1)}, bf16[6144,2048]{1,0:T(8,128)(2,1)}, ...), branch_computations={%region_1.10_spmd, %region_10.19_spmd, %region_19.28_spmd} | conditional | flops 33885274112 | bytes 549459840 | solution.py:689
  9.8 1.8 %branch_0_fun.11 = (bf16[240,384]{1,0:T(8,128)(2,1)S(1)}, bf16[240,384]{1,0:T(8,128)(2,1)S(1)}, bf16[240,384]{1,0:T(8,128)(2,1)S(1)}, bf16[240,384]{1,0:T(8,128)(2,1)S(1)}, bf16[304,384]{1,0:T(8,128)(2,1)S(1)}) custom-call(s32[8,512]{1,0:T(8,128)S(1)} %get-tuple-element.104.slot_ref.refs_7_, bf16[512,384]{1,0:T(8,128)(2,1)} %get-tuple-element.107.x_ref, ...), custom_call_target="tpu_custom_call" | custom-call | tf_op jit(solution)/shard_map/cond/branch_0_fun/pallas_call | solution.py:257
  11.7 1.6 collective-permute-start.3
  13.3 2.2 %collective-permute-start.4 = (bf16[240,384]{1,0:T(8,128)(2,1)S(1)}, bf16[240,384]{1,0:T(8,128)(2,1)S(1)}, u32[]{:S(2)}, u32[]{:S(2)}) collective-permute-start(bf16[240,384]{1,0:T(8,128)(2,1)S(1)} %get-tuple-element.114), channel_id=1, source_target_pairs={{0,12},{1,13},{2,14},{3,15},{4,0},{5,1},{6,2},{7,3},{8,4},{9,5},{1... | collective-permute-start | bytes 552968 | tf_op jit(solution)/shard_map/cond/branch_0_fun/ppermute | solution.py:131
  15.5 1.5 collective-permute-start
  17.7 8.2 %branch_0_fun.12 = (bf16[6144,2048]{1,0:T(8,128)(2,1)S(1)}, f32[8,128]{1,0:T(8,128)S(1)}) custom-call(bf16[6144,2048]{1,0:T(8,128)(2,1)} %get-tuple-element.117.w_ref, bf16[240,384]{1,0:T(8,128)(2,1)S(1)} %get-tuple-element.112.after_ref.refs_0_), custom_call_target="tpu_custom_call" | custom-call | bytes 50331648 | tf_op jit(solution)/shard_map/cond/branch_0_fun/pallas_call | solution.py:159
  26.0 1.6 collective-permute-start.6
  31.4 6.1 %branch_0_fun.13 = (f32[240,2048]{1,0:T(8,128)S(1)}, f32[240,2048]{1,0:T(8,128)S(1)}) custom-call(s32[5]{0:T(128)S(1)} %get-tuple-element.123.where_ref, bf16[240,384]{1,0:T(8,128)(2,1)} %copy-done.6, bf16[240,384]{1,0:T(8,128)(2,1)} %copy-done.64, bf16[240,384]{1,0:T(8,128)(2,1)} %copy-done.65, bf16[240,384]{1,0:T(8,128)(2,1)} %copy-done.66, ...), custom_call_target="tpu_custom_call" | custom-call | flops 15728640 | bytes 65536 | tf_op jit(solution)/shard_map/cond/branch_0_fun/pallas_call | solution.py:373
  39.7 2.0 %collective-permute-start.12 = (f32[1,512]{1,0:T(1,128)S(1)}, f32[1,512]{1,0:T(1,128)S(1)}, u32[]{:S(2)}, u32[]{:S(2)}) collective-permute-start(f32[1,512]{1,0:T(1,128)S(1)} %add_add_fusion.1), channel_id=1, source_target_pairs={{0,8},{1,9},{2,10},{3,11},{4,12},{5,13},{6,14},{7,15},{8,0},{9,1},... | collective-permute-start | bytes 6152 | tf_op jit(solution)/shard_map/cond/branch_0_fun/ppermute | solution.py:131
  41.7 1.5 collective-permute-start.13
  44.6 10.4 %branch_0_fun.14 = (f32[240,2048]{1,0:T(8,128)S(1)}, f32[240,2048]{1,0:T(8,128)S(1)}) custom-call(s32[6]{0:T(128)S(1)} %get-tuple-element.136.where_ref, bf16[480,384]{1,0:T(8,128)(2,1)} %copy-done.18, bf16[480,384]{1,0:T(8,128)(2,1)} %copy-done.26, bf16[960,384]{1,0:T(8,128)(2,1)} %copy-done.40, ...), custom_call_target="tpu_custom_call", output_to_operand_aliasing={{0}: (7, {}), {1}: (8, {})} | custom-call | flops 6039797760 | bytes 25165824 | tf_op jit(solution)/shard_map/cond/branch_0_fun/pallas_call | solution.py:373
  57.6 6.5 %branch_0_fun.15.h_ref = bf16[240,2048]{1,0:T(8,128)(2,1)S(1)} custom-call(s32[5]{0:T(128)S(1)} %get-tuple-element.106.where_ref, bf16[240,384]{1,0:T(8,128)(2,1)} %copy-done.41, bf16[240,384]{1,0:T(8,128)(2,1)} %copy-done.42, bf16[480,384]{1,0:T(8,128)(2,1)} %copy-done.51, bf16[6144,2048]{1,0:T(8,128)(2,1)S(1)} %get-tuple-element.127.refs_4_.refs_3_, ...), custom_call_target="tpu_custom_call" | custom-call | flops 3019898880 | bytes 12582912 | tf_op jit(solution)/shard_map/cond/branch_0_fun/pallas_call | solution.py:373
  64.1 12.0 %branch_0_fun.16 = (f32[480,384]{1,0:T(8,128)S(1)}, f32[480,384]{1,0:T(8,128)S(1)}, bf16[960,384]{1,0:T(8,128)(2,1)S(1)}, f32[480,384]{1,0:T(8,128)S(1)}, f32[48...) custom-call(s32[8]{0:T(128)S(1)} %get-tuple-element.111.where_ref, bf16[240,2048]{1,0:T(8,128)(2,1)S(1)} %branch_0_fun.15.h_ref, ...), custom_call_target="tpu_custom_call" | custom-call | flops 6039797760 | bytes 31064064 | tf_op jit(solution)/shard_map/cond/branch_0_fun/pallas_call | solution.py:421
  78.5 1.6 collective-permute-start.18
  80.2 9.0 %collective-permute-done.18 = bf16[480,384]{1,0:T(8,128)(2,1)S(1)} collective-permute-done((bf16[480,384]{1,0:T(8,128)(2,1)S(1)}, bf16[480,384]{1,0:T(8,128)(2,1)S(1)}, u32[]{:S(2)}, u32[]{:S(2)}) %collective-permute-start.18) | collective-permute-done | bytes 368672 | tf_op jit(solution)/shard_map/cond/branch_0_fun/ppermute | solution.py:131
  89.2 1.5 collective-permute-start.19
  92.5 6.5 %collective-permute-done.19 = bf16[480,384]{1,0:T(8,128)(2,1)S(1)} collective-permute-done((bf16[480,384]{1,0:T(8,128)(2,1)S(1)}, bf16[480,384]{1,0:T(8,128)(2,1)S(1)}, u32[]{:S(2)}, u32[]{:S(2)}) %collective-permute-start.19) | collective-permute-done | bytes 368672 | tf_op jit(solution)/shard_map/cond/branch_0_fun/ppermute | solution.py:131
  100.6 5.0 %collective-permute-done.20.e2 = bf16[240,384]{1,0:T(8,128)(2,1)S(1)} collective-permute-done((bf16[240,384]{1,0:T(8,128)(2,1)S(1)}, bf16[240,384]{1,0:T(8,128)(2,1)S(1)}, u32[]{:S(2)}, u32[]{:S(2)}) %collective-permute-start.20) | collective-permute-done | bytes 184352 | tf_op jit(solution)/shard_map/cond/branch_0_fun/ppermute | solution.py:131
  105.5 3.8 %collective-permute-done.22.e3 = bf16[240,384]{1,0:T(8,128)(2,1)S(1)} collective-permute-done((bf16[240,384]{1,0:T(8,128)(2,1)S(1)}, bf16[240,384]{1,0:T(8,128)(2,1)S(1)}, u32[]{:S(2)}, u32[]{:S(2)}) %collective-permute-start.22) | collective-permute-done | bytes 184352 | tf_op jit(solution)/shard_map/cond/branch_0_fun/ppermute | solution.py:131
  110.6 3.2 %collective-permute-start.27 = (bf16[304,384]{1,0:T(8,128)(2,1)S(1)}, bf16[304,384]{1,0:T(8,128)(2,1)S(1)}, u32[]{:S(2)}, u32[]{:S(2)}) collective-permute-start(bf16[304,384]{1,0:T(8,128)(2,1)S(1)} %get-tuple-element.162.refs_0_), channel_id=1, source_target_pairs={{0,12},{1,13},{2,14},{3,15},{4,0},{5,1},{6,2},{7,3},{8,4},{9,5},{1... | collective-permute-start | bytes 700424 | tf_op jit(solution)/shard_map/cond/branch_0_fun/ppermute | solution.py:131
  114.3 1.6 collective-permute-start.25
  116.1 8.2 %branch_0_fun.18 = (bf16[6144,2048]{1,0:T(8,128)(2,1)S(1)}, f32[8,128]{1,0:T(8,128)S(1)}) custom-call(bf16[6144,2048]{1,0:T(8,128)(2,1)} %get-tuple-element.160.w_ref, f32[1,304]{1,0:T(1,128)S(1)} %reshape.183.after_ref), custom_call_target="tpu_custom_call" | custom-call | bytes 50331648 | tf_op jit(solution)/shard_map/cond/branch_0_fun/pallas_call | solution.py:159
  127.3 1.5 collective-permute-start.31
  128.9 4.6 %branch_0_fun.19.refs_4_ = f32[304,2048]{1,0:T(8,128)S(1)} custom-call(s32[5]{0:T(128)S(1)} %get-tuple-element.123.where_ref, bf16[304,384]{1,0:T(8,128)(2,1)} %copy-done.9, bf16[304,384]{1,0:T(8,128)(2,1)} %copy-done.58, bf16[304,384]{1,0:T(8,128)(2,1)} %copy-done.59, bf16[304,384]{1,0:T(8,128)(2,1)} %copy-done.60, ...), custom_call_target="tpu_custom_call" | custom-call | flops 9961472 | bytes 32768 | tf_op jit(solution)/shard_map/cond/branch_0_fun/pallas_call | solution.py:543
  133.6 4.3 %collective-permute-done.31 = f32[1,304]{1,0:T(1,128)S(1)} collective-permute-done((f32[1,304]{1,0:T(1,128)S(1)}, f32[1,304]{1,0:T(1,128)S(1)}, u32[]{:S(2)}, u32[]{:S(2)}) %collective-permute-start.31) | collective-permute-done | bytes 1248 | tf_op jit(solution)/shard_map/cond/branch_0_fun/ppermute | solution.py:131
  138.4 2.1 %collective-permute-start.35 = (f32[1,304]{1,0:T(1,128)S(1)}, f32[1,304]{1,0:T(1,128)S(1)}, u32[]{:S(2)}, u32[]{:S(2)}) collective-permute-start(f32[1,304]{1,0:T(1,128)S(1)} %add_add_fusion.3), channel_id=1, source_target_pairs={{0,8},{1,9},{2,10},{3,11},{4,12},{5,13},{6,14},{7,15},{8,0},{9,1},... | collective-permute-start | bytes 3656 | tf_op jit(solution)/shard_map/cond/branch_0_fun/ppermute | solution.py:131
  140.6 1.7 collective-permute-start.36
  144.3 6.9 %branch_0_fun.20.refs_4_ = f32[304,2048]{1,0:T(8,128)S(1)} custom-call(s32[6]{0:T(128)S(1)} %get-tuple-element.136.where_ref, bf16[608,384]{1,0:T(8,128)(2,1)} %copy-done.16, bf16[608,384]{1,0:T(8,128)(2,1)} %copy-done.22, bf16[1216,384]{1,0:T(8,128)(2,1)} %copy-done.33, ...), custom_call_target="tpu_custom_call", output_to_operand_aliasing={{}: (5, {})} | custom-call | flops 3825205248 | bytes 12582912 | tf_op jit(solution)/shard_map/cond/branch_0_fun/pallas_call | solution.py:543
  154.0 7.0 %branch_0_fun.21 = f32[304,128]{1,0:T(8,128)} custom-call(s32[5]{0:T(128)S(1)} %get-tuple-element.106.where_ref, bf16[304,384]{1,0:T(8,128)(2,1)} %copy-done.34, bf16[304,384]{1,0:T(8,128)(2,1)} %copy-done.35, bf16[608,384]{1,0:T(8,128)(2,1)} %copy-done.45, bf16[6144,2048]{1,0:T(8,128)(2,1)S(1)} %get-tuple-element.169.refs_4_.refs_3_, ...), custom_call_target="tpu_custom_call" | custom-call | flops 1912602624 | bytes 6291456 | tf_op jit(solution)/shard_map/cond/branch_0_fun/pallas_call | solution.py:543
  163.9 3.8 %all-to-all-start = ((f32[16,3,32]{2,1,0:T(4,128)}), f32[16,3,32]{2,1,0:T(4,128)S(1)}, u32[]{:S(2)}, u32[]{:S(2)}) async-start(f32[16,3,32]{2,1,0:T(4,128)} %copy.57), calls=%async_computation | async-start | bytes 65536 | tf_op jit(solution)/shard_map/all_to_all | solution.py:712
  167.7 6.6 %all-to-all-done = f32[16,3,32]{2,1,0:T(4,128)S(1)} async-done(((f32[16,3,32]{2,1,0:T(4,128)}), f32[16,3,32]{2,1,0:T(4,128)S(1)}, u32[]{:S(2)}, u32[]{:S(2)}) %all-to-all-start) | async-done | bytes 6176 | tf_op jit(solution)/shard_map/all_to_all | solution.py:712
  (164 shorter events, 35.7 us)
Async XLA Ops:
  11.7 14.2 %collective-permute-start.3 = (bf16[240,384]{1,0:T(8,128)(2,1)S(1)}, bf16[240,384]{1,0:T(8,128)(2,1)S(1)}, u32[]{:S(2)}, u32[]{:S(2)}) collective-permute-start(bf16[240,384]{1,0:T(8,128)(2,1)S(1)} %get-tuple-element.113), channel_id=1, source_target_pairs={{0,4},{1,5},{2,6},{3,7},{4,8},{5,9},{6,10},{7,11},{8,12},{9,13},{1... | collective-permute-start | bytes 552968 | tf_op jit(solution)/shard_map/cond/branch_0_fun/ppermute | solution.py:131
  13.3 12.6 %collective-permute-start.4 = (bf16[240,384]{1,0:T(8,128)(2,1)S(1)}, bf16[240,384]{1,0:T(8,128)(2,1)S(1)}, u32[]{:S(2)}, u32[]{:S(2)}) collective-permute-start(bf16[240,384]{1,0:T(8,128)(2,1)S(1)} %get-tuple-element.114), channel_id=1, source_target_pairs={{0,12},{1,13},{2,14},{3,15},{4,0},{5,1},{6,2},{7,3},{8,4},{9,5},{1... | collective-permute-start | bytes 552968 | tf_op jit(solution)/shard_map/cond/branch_0_fun/ppermute | solution.py:131
  15.5 10.4 %collective-permute-start = (bf16[240,384]{1,0:T(8,128)(2,1)S(1)}, bf16[240,384]{1,0:T(8,128)(2,1)S(1)}, u32[]{:S(2)}, u32[]{:S(2)}) collective-permute-start(bf16[240,384]{1,0:T(8,128)(2,1)S(1)} %get-tuple-element.112.after_ref.refs_0_), channel_id=1, source_target_pairs={{0,2},{1,3},{2,0},{3,1},{4,6},{5,7},{6,4},{7,5},{8,10},{9,11},{10,... | collective-permute-start | bytes 552968 | tf_op jit(solution)/shard_map/cond/branch_0_fun/ppermute | solution.py:131
  17.1 8.9 %collective-permute-start.1 = (bf16[240,384]{1,0:T(8,128)(2,1)S(1)}, bf16[240,384]{1,0:T(8,128)(2,1)S(1)}, u32[]{:S(2)}, u32[]{:S(2)}) collective-permute-start(bf16[240,384]{1,0:T(8,128)(2,1)S(1)} %get-tuple-element.112.after_ref.refs_0_), channel_id=1, source_target_pairs={{0,1},{1,0},{2,3},{3,2},{4,5},{5,4},{6,7},{7,6},{8,9},{9,8},{10,11... | collective-permute-start | bytes 552968 | tf_op jit(solution)/shard_map/cond/branch_0_fun/ppermute | solution.py:131
  17.1 8.9 %collective-permute-start.2 = (bf16[240,384]{1,0:T(8,128)(2,1)S(1)}, bf16[240,384]{1,0:T(8,128)(2,1)S(1)}, u32[]{:S(2)}, u32[]{:S(2)}) collective-permute-start(bf16[240,384]{1,0:T(8,128)(2,1)S(1)} %get-tuple-element.112.after_ref.refs_0_), channel_id=1, source_target_pairs={{0,3},{1,2},{2,1},{3,0},{4,7},{5,6},{6,5},{7,4},{8,11},{9,10},{10,... | collective-permute-start | bytes 552968 | tf_op jit(solution)/shard_map/cond/branch_0_fun/ppermute | solution.py:131
  26.0 12.4 %collective-permute-start.6 = (bf16[480,384]{1,0:T(8,128)(2,1)S(1)}, bf16[480,384]{1,0:T(8,128)(2,1)S(1)}, u32[]{:S(2)}, u32[]{:S(2)}) collective-permute-start(bf16[480,384]{1,0:T(8,128)(2,1)S(1)} %pad_maximum_fusion.4.refs_0_), channel_id=1, source_target_pairs={{0,2},{1,3},{2,0},{3,1},{4,6},{5,7},{6,4},{7,5},{8,10},{9,11},{10,... | collective-permute-start | bytes 1105928 | tf_op jit(solution)/shard_map/cond/branch_0_fun/ppermute | solution.py:131
  28.1 10.3 %collective-permute-start.5 = (bf16[240,384]{1,0:T(8,128)(2,1)S(1)}, bf16[240,384]{1,0:T(8,128)(2,1)S(1)}, u32[]{:S(2)}, u32[]{:S(2)}) collective-permute-start(bf16[240,384]{1,0:T(8,128)(2,1)S(1)} %get-tuple-element.119), channel_id=1, source_target_pairs={{0,8},{1,9},{2,10},{3,11},{4,12},{5,13},{6,14},{7,15},{8,0},{9,1},... | collective-permute-start | bytes 552968 | tf_op jit(solution)/shard_map/cond/branch_0_fun/ppermute | solution.py:131
  29.5 8.1 %collective-permute-start.7 = (f32[1,512]{1,0:T(1,128)S(1)}, f32[1,512]{1,0:T(1,128)S(1)}, u32[]{:S(2)}, u32[]{:S(2)}) collective-permute-start(f32[1,512]{1,0:T(1,128)S(1)} %broadcast_add_fusion), channel_id=1, source_target_pairs={{0,1},{1,0},{2,3},{3,2},{4,5},{5,4},{6,7},{7,6},{8,9},{9,8},{10,11... | collective-permute-start | bytes 6152 | tf_op jit(solution)/shard_map/cond/branch_0_fun/ppermute | solution.py:131
  29.5 8.0 %collective-permute-start.8 = (f32[1,512]{1,0:T(1,128)S(1)}, f32[1,512]{1,0:T(1,128)S(1)}, u32[]{:S(2)}, u32[]{:S(2)}) collective-permute-start(f32[1,512]{1,0:T(1,128)S(1)} %broadcast_add_fusion), channel_id=1, source_target_pairs={{0,2},{1,3},{2,0},{3,1},{4,6},{5,7},{6,4},{7,5},{8,10},{9,11},{10,... | collective-permute-start | bytes 6152 | tf_op jit(solution)/shard_map/cond/branch_0_fun/ppermute | solution.py:131
  38.6 16.4 %collective-permute-start.11 = (f32[1,512]{1,0:T(1,128)S(1)}, f32[1,512]{1,0:T(1,128)S(1)}, u32[]{:S(2)}, u32[]{:S(2)}) collective-permute-start(f32[1,512]{1,0:T(1,128)S(1)} %add_add_fusion.1), channel_id=1, source_target_pairs={{0,4},{1,5},{2,6},{3,7},{4,8},{5,9},{6,10},{7,11},{8,12},{9,13},{1... | collective-permute-start | bytes 6152 | tf_op jit(solution)/shard_map/cond/branch_0_fun/ppermute | solution.py:131
  39.7 15.3 %collective-permute-start.12 = (f32[1,512]{1,0:T(1,128)S(1)}, f32[1,512]{1,0:T(1,128)S(1)}, u32[]{:S(2)}, u32[]{:S(2)}) collective-permute-start(f32[1,512]{1,0:T(1,128)S(1)} %add_add_fusion.1), channel_id=1, source_target_pairs={{0,8},{1,9},{2,10},{3,11},{4,12},{5,13},{6,14},{7,15},{8,0},{9,1},... | collective-permute-start | bytes 6152 | tf_op jit(solution)/shard_map/cond/branch_0_fun/ppermute | solution.py:131
  41.7 13.3 %collective-permute-start.13 = (f32[1,512]{1,0:T(1,128)S(1)}, f32[1,512]{1,0:T(1,128)S(1)}, u32[]{:S(2)}, u32[]{:S(2)}) collective-permute-start(f32[1,512]{1,0:T(1,128)S(1)} %add_add_fusion.1), channel_id=1, source_target_pairs={{0,12},{1,13},{2,14},{3,15},{4,0},{5,1},{6,2},{7,3},{8,4},{9,5},{1... | collective-permute-start | bytes 6152 | tf_op jit(solution)/shard_map/cond/branch_0_fun/ppermute | solution.py:131
  43.2 11.8 %collective-permute-start.10 = (bf16[240,384]{1,0:T(8,128)(2,1)S(1)}, bf16[240,384]{1,0:T(8,128)(2,1)S(1)}, u32[]{:S(2)}, u32[]{:S(2)}) collective-permute-start(bf16[240,384]{1,0:T(8,128)(2,1)S(1)} %collective-permute-done.5.refs_0_), channel_id=1, source_target_pairs={{0,2},{1,3},{2,0},{3,1},{4,6},{5,7},{6,4},{7,5},{8,10},{9,11},{10,... | collective-permute-start | bytes 552968 | tf_op jit(solution)/shard_map/cond/branch_0_fun/ppermute | solution.py:131
  78.5 10.7 %collective-permute-start.18 = (bf16[480,384]{1,0:T(8,128)(2,1)S(1)}, bf16[480,384]{1,0:T(8,128)(2,1)S(1)}, u32[]{:S(2)}, u32[]{:S(2)}) collective-permute-start(bf16[480,384]{1,0:T(8,128)(2,1)S(1)} %add_convert_fusion.2), channel_id=1, source_target_pairs={{0,2},{1,3},{2,0},{3,1},{4,6},{5,7},{6,4},{7,5},{8,10},{9,11},{10,... | collective-permute-start | bytes 1105928 | tf_op jit(solution)/shard_map/cond/branch_0_fun/ppermute | solution.py:131
  89.2 9.8 %collective-permute-start.19 = (bf16[480,384]{1,0:T(8,128)(2,1)S(1)}, bf16[480,384]{1,0:T(8,128)(2,1)S(1)}, u32[]{:S(2)}, u32[]{:S(2)}) collective-permute-start(bf16[480,384]{1,0:T(8,128)(2,1)S(1)} %add_convert_fusion.3), channel_id=1, source_target_pairs={{0,2},{1,3},{2,0},{3,1},{4,6},{5,7},{6,4},{7,5},{8,10},{9,11},{10,... | collective-permute-start | bytes 1105928 | tf_op jit(solution)/shard_map/cond/branch_0_fun/ppermute | solution.py:131
  90.9 14.6 %collective-permute-start.20 = (bf16[240,384]{1,0:T(8,128)(2,1)S(1)}, bf16[240,384]{1,0:T(8,128)(2,1)S(1)}, u32[]{:S(2)}, u32[]{:S(2)}) collective-permute-start(bf16[240,384]{1,0:T(8,128)(2,1)S(1)} %get-tuple-element.387), channel_id=1, source_target_pairs={{0,8},{1,9},{2,10},{3,11},{4,12},{5,13},{6,14},{7,15},{8,0},{9,1},... | collective-permute-start | bytes 552968 | tf_op jit(solution)/shard_map/cond/branch_0_fun/ppermute | solution.py:131
  92.3 13.2 %collective-permute-start.21 = (bf16[240,384]{1,0:T(8,128)(2,1)S(1)}, bf16[240,384]{1,0:T(8,128)(2,1)S(1)}, u32[]{:S(2)}, u32[]{:S(2)}) collective-permute-start(bf16[240,384]{1,0:T(8,128)(2,1)S(1)} %get-tuple-element.386), channel_id=1, source_target_pairs={{0,4},{1,5},{2,6},{3,7},{4,8},{5,9},{6,10},{7,11},{8,12},{9,13},{1... | collective-permute-start | bytes 552968 | tf_op jit(solution)/shard_map/cond/branch_0_fun/ppermute | solution.py:131
  99.2 10.1 %collective-permute-start.22 = (bf16[240,384]{1,0:T(8,128)(2,1)S(1)}, bf16[240,384]{1,0:T(8,128)(2,1)S(1)}, u32[]{:S(2)}, u32[]{:S(2)}) collective-permute-start(bf16[240,384]{1,0:T(8,128)(2,1)S(1)} %get-tuple-element.384), channel_id=1, source_target_pairs={{0,12},{1,13},{2,14},{3,15},{4,0},{5,1},{6,2},{7,3},{8,4},{9,5},{1... | collective-permute-start | bytes 552968 | tf_op jit(solution)/shard_map/cond/branch_0_fun/ppermute | solution.py:131
  110.0 14.4 %collective-permute-start.26 = (bf16[304,384]{1,0:T(8,128)(2,1)S(1)}, bf16[304,384]{1,0:T(8,128)(2,1)S(1)}, u32[]{:S(2)}, u32[]{:S(2)}) collective-permute-start(bf16[304,384]{1,0:T(8,128)(2,1)S(1)} %get-tuple-element.162.refs_0_), channel_id=1, source_target_pairs={{0,4},{1,5},{2,6},{3,7},{4,8},{5,9},{6,10},{7,11},{8,12},{9,13},{1... | collective-permute-start | bytes 700424 | tf_op jit(solution)/shard_map/cond/branch_0_fun/ppermute | solution.py:131
  110.6 13.7 %collective-permute-start.27 = (bf16[304,384]{1,0:T(8,128)(2,1)S(1)}, bf16[304,384]{1,0:T(8,128)(2,1)S(1)}, u32[]{:S(2)}, u32[]{:S(2)}) collective-permute-start(bf16[304,384]{1,0:T(8,128)(2,1)S(1)} %get-tuple-element.162.refs_0_), channel_id=1, source_target_pairs={{0,12},{1,13},{2,14},{3,15},{4,0},{5,1},{6,2},{7,3},{8,4},{9,5},{1... | collective-permute-start | bytes 700424 | tf_op jit(solution)/shard_map/cond/branch_0_fun/ppermute | solution.py:131
  113.8 10.6 %collective-permute-start.23 = (bf16[304,384]{1,0:T(8,128)(2,1)S(1)}, bf16[304,384]{1,0:T(8,128)(2,1)S(1)}, u32[]{:S(2)}, u32[]{:S(2)}) collective-permute-start(bf16[304,384]{1,0:T(8,128)(2,1)S(1)} %get-tuple-element.162.refs_0_), channel_id=1, source_target_pairs={{0,2},{1,3},{2,0},{3,1},{4,6},{5,7},{6,4},{7,5},{8,10},{9,11},{10,... | collective-permute-start | bytes 700424 | tf_op jit(solution)/shard_map/cond/branch_0_fun/ppermute | solution.py:131
  114.3 10.1 %collective-permute-start.24 = (bf16[304,384]{1,0:T(8,128)(2,1)S(1)}, bf16[304,384]{1,0:T(8,128)(2,1)S(1)}, u32[]{:S(2)}, u32[]{:S(2)}) collective-permute-start(bf16[304,384]{1,0:T(8,128)(2,1)S(1)} %get-tuple-element.162.refs_0_), channel_id=1, source_target_pairs={{0,1},{1,0},{2,3},{3,2},{4,5},{5,4},{6,7},{7,6},{8,9},{9,8},{10,11... | collective-permute-start | bytes 700424 | tf_op jit(solution)/shard_map/cond/branch_0_fun/ppermute | solution.py:131
  114.3 10.1 %collective-permute-start.25 = (bf16[304,384]{1,0:T(8,128)(2,1)S(1)}, bf16[304,384]{1,0:T(8,128)(2,1)S(1)}, u32[]{:S(2)}, u32[]{:S(2)}) collective-permute-start(bf16[304,384]{1,0:T(8,128)(2,1)S(1)} %get-tuple-element.162.refs_0_), channel_id=1, source_target_pairs={{0,3},{1,2},{2,1},{3,0},{4,7},{5,6},{6,5},{7,4},{8,11},{9,10},{10,... | collective-permute-start | bytes 700424 | tf_op jit(solution)/shard_map/cond/branch_0_fun/ppermute | solution.py:131
  124.5 13.7 %collective-permute-start.29 = (bf16[608,384]{1,0:T(8,128)(2,1)S(1)}, bf16[608,384]{1,0:T(8,128)(2,1)S(1)}, u32[]{:S(2)}, u32[]{:S(2)}) collective-permute-start(bf16[608,384]{1,0:T(8,128)(2,1)S(1)} %pad_maximum_fusion.2.refs_0_), channel_id=1, source_target_pairs={{0,2},{1,3},{2,0},{3,1},{4,6},{5,7},{6,4},{7,5},{8,10},{9,11},{10,... | collective-permute-start | bytes 1400840 | tf_op jit(solution)/shard_map/cond/branch_0_fun/ppermute | solution.py:131
  125.4 12.7 %collective-permute-start.28 = (bf16[304,384]{1,0:T(8,128)(2,1)S(1)}, bf16[304,384]{1,0:T(8,128)(2,1)S(1)}, u32[]{:S(2)}, u32[]{:S(2)}) collective-permute-start(bf16[304,384]{1,0:T(8,128)(2,1)S(1)} %get-tuple-element.162.refs_0_), channel_id=1, source_target_pairs={{0,8},{1,9},{2,10},{3,11},{4,12},{5,13},{6,14},{7,15},{8,0},{9,1},... | collective-permute-start | bytes 700424 | tf_op jit(solution)/shard_map/cond/branch_0_fun/ppermute | solution.py:131
  127.3 10.6 %collective-permute-start.31 = (f32[1,304]{1,0:T(1,128)S(1)}, f32[1,304]{1,0:T(1,128)S(1)}, u32[]{:S(2)}, u32[]{:S(2)}) collective-permute-start(f32[1,304]{1,0:T(1,128)S(1)} %broadcast_add_fusion.5), channel_id=1, source_target_pairs={{0,2},{1,3},{2,0},{3,1},{4,6},{5,7},{6,4},{7,5},{8,10},{9,11},{10,... | collective-permute-start | bytes 3656 | tf_op jit(solution)/shard_map/cond/branch_0_fun/ppermute | solution.py:131
  128.8 9.3 %collective-permute-start.32 = (f32[1,304]{1,0:T(1,128)S(1)}, f32[1,304]{1,0:T(1,128)S(1)}, u32[]{:S(2)}, u32[]{:S(2)}) collective-permute-start(f32[1,304]{1,0:T(1,128)S(1)} %broadcast_add_fusion.5), channel_id=1, source_target_pairs={{0,3},{1,2},{2,1},{3,0},{4,7},{5,6},{6,5},{7,4},{8,11},{9,10},{10,... | collective-permute-start | bytes 3656 | tf_op jit(solution)/shard_map/cond/branch_0_fun/ppermute | solution.py:131
  138.4 12.8 %collective-permute-start.34 = (f32[1,304]{1,0:T(1,128)S(1)}, f32[1,304]{1,0:T(1,128)S(1)}, u32[]{:S(2)}, u32[]{:S(2)}) collective-permute-start(f32[1,304]{1,0:T(1,128)S(1)} %add_add_fusion.3), channel_id=1, source_target_pairs={{0,4},{1,5},{2,6},{3,7},{4,8},{5,9},{6,10},{7,11},{8,12},{9,13},{1... | collective-permute-start | bytes 3656 | tf_op jit(solution)/shard_map/cond/branch_0_fun/ppermute | solution.py:131
  138.4 12.8 %collective-permute-start.35 = (f32[1,304]{1,0:T(1,128)S(1)}, f32[1,304]{1,0:T(1,128)S(1)}, u32[]{:S(2)}, u32[]{:S(2)}) collective-permute-start(f32[1,304]{1,0:T(1,128)S(1)} %add_add_fusion.3), channel_id=1, source_target_pairs={{0,8},{1,9},{2,10},{3,11},{4,12},{5,13},{6,14},{7,15},{8,0},{9,1},... | collective-permute-start | bytes 3656 | tf_op jit(solution)/shard_map/cond/branch_0_fun/ppermute | solution.py:131
  140.6 10.7 %collective-permute-start.36 = (f32[1,304]{1,0:T(1,128)S(1)}, f32[1,304]{1,0:T(1,128)S(1)}, u32[]{:S(2)}, u32[]{:S(2)}) collective-permute-start(f32[1,304]{1,0:T(1,128)S(1)} %add_add_fusion.3), channel_id=1, source_target_pairs={{0,12},{1,13},{2,14},{3,15},{4,0},{5,1},{6,2},{7,3},{8,4},{9,5},{1... | collective-permute-start | bytes 3656 | tf_op jit(solution)/shard_map/cond/branch_0_fun/ppermute | solution.py:131
  142.3 9.0 %collective-permute-start.33 = (bf16[304,384]{1,0:T(8,128)(2,1)S(1)}, bf16[304,384]{1,0:T(8,128)(2,1)S(1)}, u32[]{:S(2)}, u32[]{:S(2)}) collective-permute-start(bf16[304,384]{1,0:T(8,128)(2,1)S(1)} %collective-permute-done.28.refs_0_), channel_id=1, source_target_pairs={{0,2},{1,3},{2,0},{3,1},{4,6},{5,7},{6,4},{7,5},{8,10},{9,11},{10,... | collective-permute-start | bytes 700424 | tf_op jit(solution)/shard_map/cond/branch_0_fun/ppermute | solution.py:131
  163.9 10.4 %all-to-all-start = ((f32[16,3,32]{2,1,0:T(4,128)}), f32[16,3,32]{2,1,0:T(4,128)S(1)}, u32[]{:S(2)}, u32[]{:S(2)}) async-start(f32[16,3,32]{2,1,0:T(4,128)} %copy.57), calls=%async_computation | async-start | bytes 65536 | tf_op jit(solution)/shard_map/all_to_all | solution.py:712
  (33 other events, 187.6 us)
